TPU v7x, 32 devices: a whole 2x2x4 slice. The times are simulated.
32 devices in a mesh: row: 8 (over z, y), col: 4 (over x, core).
Axes of the slice: x: 2, y: 2, z: 4, core: 2. Of those that a mesh axis runs over, the one named last changes fastest.
Arguments:
- trail_adjoint: float32 [4096, 4096], P('row', 'col'), may hold values from -6 to 6
- lower_new: float32 [4096, 256], P('row', 'col'), may hold values from -0.09375 to 0.09375
- upper_new: float32 [256, 4096], P('row', 'col'), may hold values from -0.09375 to 0.09375
- lower_old_top: float32 [256, 256], replicated, may hold values from -0.375 to 0.375
- lower_old: float32 [4096, 256], P('row', 'col'), may hold values from -0.09375 to 0.09375
- upper_old_left: float32 [256, 256], replicated, may hold values from -0.375 to 0.375
- upper_old: float32 [256, 4096], P('row', 'col'), may hold values from -0.09375 to 0.09375
- diag_lower_new: float32 [256, 256], replicated, as said below
- diag_upper_new: float32 [256, 256], replicated, as said below
- inverse_lower_new: float32 [256, 256], replicated, as said below
- inverse_upper_new: float32 [256, 256], replicated, as said below
- diag_lower_old: float32 [256, 256], replicated, as said below
- diag_upper_old: float32 [256, 256], replicated, as said below
- inverse_lower_old: float32 [256, 256], replicated, as said below
- inverse_upper_old: float32 [256, 256], replicated, as said below
Outputs:
- corner_old: float32 [256, 256], replicated
- strip_top: float32 [256, 256], replicated
- strip_bottom: float32 [4096, 256], P(('row', 'col'))
- band_left: float32 [256, 256], replicated
- band_right: float32 [256, 4096], P(None, 'col')
Inputs may be any that keep to these rules, and one draw needn't show every extreme that they name: `diag_lower_new`: unit lower triangular. `diag_upper_new`: upper triangular, diagonal from 1 to 2. `inverse_lower_new`: the inverse of diag_lower_new. `inverse_upper_new`: the inverse of diag_upper_new. `diag_lower_old`: unit lower triangular. `diag_upper_old`: upper triangular, diagonal from 1 to 2. `inverse_lower_old`: the inverse of diag_lower_old. `inverse_upper_old`: the inverse of diag_upper_old.
All inputs are finite; a program needn't handle non-finite values.
Results may differ from a plain program's by a relative error of at most 0.000075.
Values sent between devices are 32-bit elements; how exact they have to be, the bound alone decides.
A program may use at most 128 MiB of HBM per device.

v0:
```python
import functools

import jax
import jax.numpy as jnp
from jax import lax
from jax.experimental import pallas as pl
from jax.experimental.pallas import tpu as pltpu
from jax.sharding import PartitionSpec as P

f32, bf16 = jnp.float32, jnp.bfloat16
NN, NT = ((1,), (0,)), ((1,), (1,))


def split(x):
    high = x.astype(bf16)
    return high, (x - high.astype(f32)).astype(bf16)


def mul(a, b, dims=NN):
    def one(x, y):
        return lax.dot_general(x, y, (dims, ((), ())), preferred_element_type=f32)

    return one(a[0], b[0]) + (one(a[0], b[1]) + one(a[1], b[0]))


def start(axis, n, me, source, target, send, recv):
    copies = []
    for d in range(1, n):
        peer = lax.rem(me + d, n)
        copy = pltpu.make_async_remote_copy(
            src_ref=source(peer),
            dst_ref=target,
            send_sem=send.at[d],
            recv_sem=recv.at[d],
            device_id={axis: peer},
            device_id_type=pl.DeviceIdType.MESH,
        )
        copy.start()
        copies.append(copy)
    return copies


def arrive(copies):
    for copy in copies:
        copy.wait_recv()


def kernel(
    nr, nc, ny, a_hbm, un_ref, uo_ref, l_ref, lot_hbm, uol_hbm, iln_hbm, iun_hbm, ilo_hbm, iuo_hbm,
    strip_ref, band_ref, both_ref, left_ref,
    a_ref, ah, al, xu, xl, ut, lt, pb, ps, ry, sz, rz, rp, bc, uni, lni,
    pa, ra, sa, ta, ga, pl_, rl, sl, tl, gl,
    sq, asem, qsem, rs_send, rs_recv, cs_send, cs_recv,
):
    r, c = lax.axis_index("row"), lax.axis_index("col")
    rows, cols = a_hbm.shape
    wu, wl = cols // nr, rows // nc
    width = iln_hbm.shape[0]
    hl = width // nc
    nz = nr // ny
    z, y = r // ny, lax.rem(r, ny)
    far = [nz // 2] * (nz > 1) + [k for k in range(nz - 1, 0, -1) if k != nz // 2]
    load = pltpu.make_async_copy(a_hbm, a_ref, asem)
    squares = (iuo_hbm, uol_hbm, iun_hbm, iln_hbm, lot_hbm, ilo_hbm)
    loads = [pltpu.make_async_copy(m, sq.at[i], qsem.at[i]) for i, m in enumerate(squares)]
    for copy in loads:
        copy.start()
    load.start()
    barrier = pltpu.get_barrier_semaphore()
    for d in range(1, nr):
        pl.semaphore_signal(barrier, inc=1, device_id={"row": lax.rem(r + d, nr)}, device_id_type=pl.DeviceIdType.MESH)
    for d in range(1, nc):
        pl.semaphore_signal(barrier, inc=1, device_id={"col": lax.rem(c + d, nc)}, device_id_type=pl.DeviceIdType.MESH)
    pl.semaphore_wait(barrier, nr + nc - 2)

    def ucol(i):
        return pl.ds(pl.multiple_of(i * wu, wu), wu)

    def lcol(i):
        return pl.ds(pl.multiple_of(i * wl, wl), wl)

    sent = []

    def row_stage(k, source, target):
        copies = start("row", nr, r, source, target, rs_send.at[k], rs_recv.at[k])
        sent.extend(copies)
        return copies

    def col_stage(k, source, target):
        copies = start("col", nc, c, source, target, cs_send.at[k], cs_recv.at[k])
        sent.extend(copies)
        return copies

    def push(stage, index, source, target, zi, yi):
        copy = pltpu.make_async_remote_copy(
            src_ref=source,
            dst_ref=target,
            send_sem=rs_send.at[stage, index],
            recv_sem=rs_recv.at[stage, index],
            device_id={"row": zi * ny + yi},
            device_id_type=pl.DeviceIdType.MESH,
        )
        copy.start()
        sent.append(copy)
        return copy

    def across(stage, k, source, slot):
        return [push(stage, k * ny + d, source, slot, z, lax.rem(y + d, ny)) for d in range(1, ny)]

    def gather_start(stage, source, slot):
        along = {k: push(stage, k, source, slot(r), lax.rem(z + k, nz), y) for k in far}
        return along, across(stage + 1, 0, source, slot(r))

    def gather_pass(stage, state, slot):
        along, over = state
        for k in far[::-1]:
            along[k].wait_recv()
            here = slot(lax.rem(z - k + nz, nz) * ny + y)
            over.extend(across(stage + 1, k, here, here))
        return over

    cores = 2 if nc % 2 == 0 else 1
    nx = nc // cores
    x, core = c // cores, lax.rem(c, cores)

    def toss(stage, index, source, target, peer):
        copy = pltpu.make_async_remote_copy(
            src_ref=source,
            dst_ref=target,
            send_sem=cs_send.at[stage, index],
            recv_sem=cs_recv.at[stage, index],
            device_id={"col": peer},
            device_id_type=pl.DeviceIdType.MESH,
        )
        copy.start()
        sent.append(copy)
        return copy

    def twin(stage, k, source, target):
        if cores == 1:
            return []
        return [toss(stage, nx + k, source, target, x * cores + 1 - core)]

    def spread_start(stage, source, slot):
        along = [toss(stage, k, source, slot(c), lax.rem(x + k, nx) * cores + core) for k in range(1, nx)]
        return along, twin(stage, 0, source, slot(c))

    def spread_end(stage, state, slot):
        along, near = state
        for k in range(1, nx):
            along[k - 1].wait_recv()
            here = slot(lax.rem(x - k + nx, nx) * cores + core)
            near = near + twin(stage, k, here, here)
        return near

    u0 = row_stage(0, lambda p: un_ref.at[:, ucol(p)], xu.at[0, r])
    u0 = u0 + row_stage(11, lambda p: uo_ref.at[:, ucol(p)], xu.at[1, r])
    l0 = col_stage(0, lambda p: l_ref.at[:, lcol(p)], xl.at[c])
    xu[0, r] = un_ref[:, ucol(r)]
    xu[1, r] = uo_ref[:, ucol(r)]
    xl[c] = l_ref[:, lcol(c)]
    for copy in loads:
        copy.wait()
    iuo, iun = split(sq[0]), split(sq[2])
    mix_u = split(mul(split(mul(iuo, split(sq[1]))), iun))
    ilo = sq[5]
    mix_l = mul(split(mul(split(sq[3]), split(sq[4]))), split(ilo))
    mix_l, ilo, iln = split(mix_l.T), split(ilo.T), split(sq[3].T)
    arrive(u0)
    un = split(xu[0].reshape(width, wu))
    ut[:, ucol(r)] = mul(iuo, split(xu[1].reshape(width, wu))) - mul(mix_u, un)
    uslot = lambda i: ut.at[:, ucol(i)]
    u1 = gather_start(1, uslot(r), uslot)
    arrive(l0)
    ln = split(xl[:, :hl].reshape(width, wl))
    lt[:, lcol(c)] = mul(ilo, split(xl[:, hl:].reshape(width, wl))) - mul(mix_l, ln)
    lslot = lambda i: lt.at[:, lcol(i)]
    l1 = spread_start(1, lslot(c), lslot)
    uni[...] = mul(iun, un)
    lni[...] = mul(iln, ln)
    load.wait()
    high, low = split(a_ref[...])
    ah[...] = high
    al[...] = low
    arrive(spread_end(1, l1, lslot))
    lts = split(lt[...])
    tile = 2 * wu
    for i in range(cols // tile):
        here = slice(i * tile, (i + 1) * tile)
        pb[:, here] = -mul(lts, (ah[:, here], al[:, here]))
    b0 = {}
    for k in far + [0]:
        zt = lax.rem(z + k, nz)
        b0[k] = [
            push(3, k * ny + d, pb.at[:, ucol(zt * ny + lax.rem(y + d, ny))], ry.at[k, d], z, lax.rem(y + d, ny))
            for d in range(1, ny)
        ]
    over = gather_pass(1, u1, uslot)
    b1 = {}
    for k in far + [0]:
        arrive(b0[k])
        zt = lax.rem(z + k, nz)
        total = pb[:, ucol(zt * ny + y)]
        for d in range(1, ny):
            total = total + ry[k, d]
        if k:
            sz[k] = total
            b1[k] = push(4, k, sz.at[k], rz.at[k], zt, y)
        else:
            rz[0] = total
    arrive(over)
    uts = split(ut[...])
    tile = 2 * wl
    for i in range(rows // tile):
        here = slice(i * tile, (i + 1) * tile)
        ps[here] = -mul((ah[here], al[here]), uts, NT)
    p0 = col_stage(2, lambda p: ps.at[lcol(p)], rp.at[c])
    rp[c] = ps[lcol(c)]

    def small_cols(stage, part, got):
        high = part.shape[0] // nc
        at = lambda p: part.at[pl.ds(pl.multiple_of(p * high, high), high)]
        copies = col_stage(stage, at, got.at[c])
        got[c] = part[pl.ds(pl.multiple_of(c * high, high), high)]
        return copies

    def small_rows(stage, copies, got, send, take):
        arrive(copies)
        total = got[0]
        for i in range(1, nc):
            total = total + got[i]
        each = send.shape[1]
        for i in range(nr):
            send[i] = total[i * each : (i + 1) * each]
        copies = row_stage(stage, lambda p: send.at[p], take.at[r])
        take[r] = send[r]
        return copies

    def back_rows(stage, copies, take, whole):
        arrive(copies)
        total = take[0]
        for i in range(1, nr):
            total = total + take[i]
        whole[r] = total
        return row_stage(stage, lambda p: whole.at[r], whole.at[r])

    def back_cols(stage, copies, whole, out):
        arrive(copies)
        copies = spread_start(stage, whole, lambda i: out.at[i])
        out[c] = whole[...]
        return copies

    arrive([b1[k] for k in far])
    band = rz[0]
    for k in range(1, nz):
        band = band + rz[k]
    bc[...] = band
    bslot = lambda i: band_ref.at[:, ucol(i)]
    b2 = gather_start(5, bc, bslot)
    band_ref[:, ucol(r)] = band
    pl_[...] = -mul(split(band), split(uni[...]), NT)
    left = small_cols(3, pl_, rl)
    arrive(p0)
    strip = rp[0]
    for i in range(1, nc):
        strip = strip + rp[i]
    strip_ref[...] = strip
    strip = split(strip)
    pa[:width] = -mul(split(lni[...]), strip)
    pa[width:] = -mul(split(lt[:, lcol(c)]), strip)
    both = small_cols(4, pa, ra)
    left = small_rows(7, left, rl, sl, tl)
    both = small_rows(8, both, ra, sa, ta)
    over = gather_pass(5, b2, bslot)
    left = back_rows(9, left, tl, gl)
    both = back_rows(10, both, ta, ga)
    left = back_cols(5, left, gl, left_ref)
    both = back_cols(6, both, ga, both_ref)
    left = spread_end(5, left, lambda i: left_ref.at[i])
    both = spread_end(6, both, lambda i: both_ref.at[i])
    arrive(left)
    arrive(both)
    arrive(over)
    for copy in sent:
        copy.wait_send()


def body(an, ln, un, lot, lo, uol, uo, dln, dun, iln, iun, dlo, duo, ilo, iuo):
    nr, nc = lax.axis_size("row"), lax.axis_size("col")
    rows, cols = an.shape
    width = iln.shape[0]
    wu, wl = cols // nr, rows // nc
    l = jnp.concatenate((ln, lo), axis=1).T
    ny = nc // 2 if nc % 2 == 0 and nr % max(nc // 2, 1) == 0 else 1
    nz = nr // ny
    vm = pl.BlockSpec(memory_space=pltpu.VMEM)
    hbm = pl.BlockSpec(memory_space=pl.ANY)
    V = pltpu.VMEM

    def chain(size):
        high = size // nc
        whole = V((nr, high // nr, width), f32)
        return [V((size, width), f32), V((nc, high, width), f32), whole, whole, whole]

    D = pltpu.SemaphoreType.DMA
    strip, band, both, left = pl.pallas_call(
        functools.partial(kernel, nr, nc, ny),
        out_shape=(
            jax.ShapeDtypeStruct((wl, width), f32),
            jax.ShapeDtypeStruct((width, cols), f32),
            jax.ShapeDtypeStruct((nc, nr, 2 * width // nc // nr, width), f32),
            jax.ShapeDtypeStruct((nc, nr, width // nc // nr, width), f32),
        ),
        in_specs=[hbm, vm, vm, vm] + [hbm] * 6,
        out_specs=(vm, vm, vm, vm),
        scratch_shapes=[
            V((rows, cols), f32), V((rows, cols), bf16), V((rows, cols), bf16),
            V((2, nr, width // nr, wu), f32), V((nc, 2 * width // nc, wl), f32),
            V((width, cols), f32), V((width, rows), f32),
            V((width, cols), f32), V((rows, width), f32),
            V((nz, ny, width, wu), f32), V((nz, width, wu), f32), V((nz, width, wu), f32),
            V((nc, wl, width), f32), V((width, wu), f32),
            V((width, wu), f32), V((width, wl), f32),
            *chain(2 * width), *chain(width),
            V((6, width, width), f32), D, D((6,)), D((12, nr)), D((12, nr)), D((7, nc)), D((7, nc)),
        ],
        compiler_params=pltpu.CompilerParams(collective_id=0, has_side_effects=True),
    )(an, un, uo, l, lot, uol, iln, iun, ilo, iuo)
    both = both.reshape(2 * width, width)
    return both[width:], both[:width], strip, left.reshape(width, width), band


def solution(mesh):
    two, whole = P("row", "col"), P()
    return jax.shard_map(
        body,
        mesh=mesh,
        in_specs=(two, two, two, whole, two, whole, two) + (whole,) * 8,
        out_specs=(P(), P(), P(("row", "col"), None), P(), P(None, "col")),
        check_vma=False,
    )
```

profile of v0, /device:TPU:0, one launch (start us, length us, event | category | flops | bytes accessed | tf_op | source)
XLA Modules:
  0.0 88.0 jit_solution(2285980333057036491)
XLA Ops:
  0.6 1.7 %maximum_bitcast_fusion.l_ref = f32[128,512]{1,0:T(8,128)} fusion(f32[512,64]{0,1:T(8,128)} %param.19, f32[512,64]{0,1:T(8,128)} %param.16), kind=kLoop, calls=%fused_computation | loop fusion | flops 65536 | bytes 524288 | tf_op jit(solution)/shard_map/transpose | solution.py:293
  2.3 79.5 %shard_map.146 = (f32[128,256]{1,0:T(8,128)}, f32[256,1024]{1,0:T(8,128)}, f32[4,8,16,256]{3,2,1,0:T(8,128)}, f32[4,8,8,256]{3,2,1,0:T(8,128)}) custom-call(f32[512,1024]{1,0:T(8,128)} %a_hbm.1, f32[32,1024]{1,0:T(8,128)} %un_ref.1, f32[32,1024]{1,0:T(8,128)} %uo_ref.1, f32[128,512]{1,0:T(8,128)} %maximum_bitcast_fusion.l_ref, f32[256,256]{1,0:T(8,128)} %lot_hbm.1, ...), custom_call_target="tpu_custom_call" | custom-call | tf_op jit(solution)/shard_map/pallas_call | solution.py:306
  81.8 0.0 copy-start
  81.8 1.9 %fusion = (f32[2,8,16,256]{3,2,1,0:T(8,128)}, f32[2,8,16,256]{3,2,1,0:T(8,128)}) fusion(f32[4,8,16,256]{3,2,1,0:T(8,128)} %get-tuple-element.9), kind=kLoop, calls=%fused_computation.1 | loop fusion | bytes 1048576 | tf_op jit(solution)/shard_map/slice | solution.py:330
  83.8 1.6 %copy.19 = f32[128,256]{1,0:T(8,128)} copy(f32[128,256]{1,0:T(8,128)} %get-tuple-element.22) | data formatting | bytes 262144
  85.3 1.7 %copy.20 = f32[256,256]{1,0:T(8,128)} copy(f32[256,256]{1,0:T(8,128)} %bitcast.5) | data formatting | bytes 524288
  87.0 0.0 copy-done
  87.0 1.0 %copy.21 = f32[256,1024]{1,0:T(8,128)} copy(f32[256,1024]{1,0:T(8,128)S(1)} %copy-done) | data formatting | bytes 2097152
Async XLA Ops:
  81.8 5.2 %copy-start = (f32[256,1024]{1,0:T(8,128)S(1)}, f32[256,1024]{1,0:T(8,128)}, u32[]{:S(2)}) copy-start(f32[256,1024]{1,0:T(8,128)} %get-tuple-element.24) | copy-start | bytes 3145732
where the time goes:
time: 88.2 us; the launch traced here: 88 us
  Pallas kernels  79.5 us (90%)
  local copies, waits for them, and re-layouts  6.15 us (7%)
  other arithmetic  1.69 us (2%)
    pallas_call x1, Pallas kernels, body(): pl.pallas_call(functools.partial(kernel, nr, nc, ny), out_shape=(jax.Shap...  79.5 us
    unnamed x5, local copies, waits for them, and re-layouts  4.21 us
    slice x1, local copies, waits for them, and re-layouts, body(): return (both[width:], both[:width], strip, left.reshape(width, width), band)  1.94 us

commit v1 on v0

--- a/solution.py
+++ b/solution.py
@@ -8,6 +8,7 @@
 from jax.sharding import PartitionSpec as P
 
 f32, bf16 = jnp.float32, jnp.bfloat16
+LIMIT = 48 << 20
 NN, NT = ((1,), (0,)), ((1,), (1,))
 
 
@@ -46,11 +47,11 @@
 
 
 def kernel(
-    nr, nc, ny, a_hbm, un_ref, uo_ref, l_ref, lot_hbm, uol_hbm, iln_hbm, iun_hbm, ilo_hbm, iuo_hbm,
+    nr, nc, ny, a_hbm, un_ref, uo_ref, ln_ref, lo_ref, lot_hbm, uol_hbm, iln_hbm, iun_hbm, ilo_hbm, iuo_hbm,
     strip_ref, band_ref, both_ref, left_ref,
     a_ref, ah, al, xu, xl, ut, lt, pb, ps, ry, sz, rz, rp, bc, uni, lni,
     pa, ra, sa, ta, ga, pl_, rl, sl, tl, gl,
-    sq, asem, qsem, rs_send, rs_recv, cs_send, cs_recv,
+    sq, asem, qsem, osem, rs_send, rs_recv, cs_send, cs_recv,
 ):
     r, c = lax.axis_index("row"), lax.axis_index("col")
     rows, cols = a_hbm.shape
@@ -63,7 +64,13 @@
     load = pltpu.make_async_copy(a_hbm, a_ref, asem)
     squares = (iuo_hbm, uol_hbm, iun_hbm, iln_hbm, lot_hbm, ilo_hbm)
     loads = [pltpu.make_async_copy(m, sq.at[i], qsem.at[i]) for i, m in enumerate(squares)]
-    for copy in loads:
+    own = [
+        pltpu.make_async_copy(un_ref.at[:, pl.ds(pl.multiple_of(r * wu, wu), wu)], xu.at[0, r], osem.at[0]),
+        pltpu.make_async_copy(uo_ref.at[:, pl.ds(pl.multiple_of(r * wu, wu), wu)], xu.at[1, r], osem.at[1]),
+        pltpu.make_async_copy(ln_ref.at[:, pl.ds(pl.multiple_of(c * wl, wl), wl)], xl.at[0, c], osem.at[2]),
+        pltpu.make_async_copy(lo_ref.at[:, pl.ds(pl.multiple_of(c * wl, wl), wl)], xl.at[1, c], osem.at[3]),
+    ]
+    for copy in own + loads:
         copy.start()
     load.start()
     barrier = pltpu.get_barrier_semaphore()
@@ -155,27 +162,25 @@
 
     u0 = row_stage(0, lambda p: un_ref.at[:, ucol(p)], xu.at[0, r])
     u0 = u0 + row_stage(11, lambda p: uo_ref.at[:, ucol(p)], xu.at[1, r])
-    l0 = col_stage(0, lambda p: l_ref.at[:, lcol(p)], xl.at[c])
-    xu[0, r] = un_ref[:, ucol(r)]
-    xu[1, r] = uo_ref[:, ucol(r)]
-    xl[c] = l_ref[:, lcol(c)]
-    for copy in loads:
+    l0 = col_stage(0, lambda p: ln_ref.at[:, lcol(p)], xl.at[0, c])
+    l0 = l0 + col_stage(7, lambda p: lo_ref.at[:, lcol(p)], xl.at[1, c])
+    for copy in own + loads:
         copy.wait()
     iuo, iun = split(sq[0]), split(sq[2])
     mix_u = split(mul(split(mul(iuo, split(sq[1]))), iun))
     ilo = sq[5]
     mix_l = mul(split(mul(split(sq[3]), split(sq[4]))), split(ilo))
     mix_l, ilo, iln = split(mix_l.T), split(ilo.T), split(sq[3].T)
+    uslot = lambda i: ut.at[:, ucol(i)]
+    lslot = lambda i: lt.at[:, lcol(i)]
+    arrive(l0)
+    ln = split(xl[0].reshape(width, wl))
+    lt[:, lcol(c)] = mul(ilo, split(xl[1].reshape(width, wl))) - mul(mix_l, ln)
+    l1 = spread_start(1, lslot(c), lslot)
     arrive(u0)
     un = split(xu[0].reshape(width, wu))
     ut[:, ucol(r)] = mul(iuo, split(xu[1].reshape(width, wu))) - mul(mix_u, un)
-    uslot = lambda i: ut.at[:, ucol(i)]
-    u1 = gather_start(1, uslot(r), uslot)
-    arrive(l0)
-    ln = split(xl[:, :hl].reshape(width, wl))
-    lt[:, lcol(c)] = mul(ilo, split(xl[:, hl:].reshape(width, wl))) - mul(mix_l, ln)
-    lslot = lambda i: lt.at[:, lcol(i)]
-    l1 = spread_start(1, lslot(c), lslot)
+    along, over = gather_start(1, uslot(r), uslot)
     uni[...] = mul(iun, un)
     lni[...] = mul(iln, ln)
     load.wait()
@@ -184,18 +189,21 @@
     al[...] = low
     arrive(spread_end(1, l1, lslot))
     lts = split(lt[...])
-    tile = 2 * wu
-    for i in range(cols // tile):
-        here = slice(i * tile, (i + 1) * tile)
-        pb[:, here] = -mul(lts, (ah[:, here], al[:, here]))
     b0 = {}
+    later = far[::-1]
     for k in far + [0]:
         zt = lax.rem(z + k, nz)
+        here = pl.ds(pl.multiple_of(zt * ny * wu, ny * wu), ny * wu)
+        pb[:, here] = -mul(lts, (ah[:, here], al[:, here]))
         b0[k] = [
             push(3, k * ny + d, pb.at[:, ucol(zt * ny + lax.rem(y + d, ny))], ry.at[k, d], z, lax.rem(y + d, ny))
             for d in range(1, ny)
         ]
-    over = gather_pass(1, u1, uslot)
+        if later:
+            m = later.pop(0)
+            along[m].wait_recv()
+            at = uslot(lax.rem(z - m + nz, nz) * ny + y)
+            over.extend(across(2, m, at, at))
     b1 = {}
     for k in far + [0]:
         arrive(b0[k])
@@ -285,16 +293,28 @@
         copy.wait_send()
 
 
+def finish(strip_ref, band_ref, both_ref, left_ref, corner, top, bottom, left, right, sem):
+    width = left_ref.shape[0]
+    pairs = (
+        (band_ref, right), (strip_ref, bottom), (left_ref, left),
+        (both_ref.at[pl.ds(width, width)], corner), (both_ref.at[pl.ds(0, width)], top),
+    )
+    copies = [pltpu.make_async_copy(source, target, sem.at[i]) for i, (source, target) in enumerate(pairs)]
+    for copy in copies:
+        copy.start()
+    for copy in copies:
+        copy.wait()
+
+
 def body(an, ln, un, lot, lo, uol, uo, dln, dun, iln, iun, dlo, duo, ilo, iuo):
     nr, nc = lax.axis_size("row"), lax.axis_size("col")
     rows, cols = an.shape
     width = iln.shape[0]
     wu, wl = cols // nr, rows // nc
-    l = jnp.concatenate((ln, lo), axis=1).T
     ny = nc // 2 if nc % 2 == 0 and nr % max(nc // 2, 1) == 0 else 1
     nz = nr // ny
     vm = pl.BlockSpec(memory_space=pltpu.VMEM)
-    hbm = pl.BlockSpec(memory_space=pl.ANY)
+    hbm = pl.BlockSpec(memory_space=pltpu.HBM)
     V = pltpu.VMEM
 
     def chain(size):
@@ -303,31 +323,40 @@
         return [V((size, width), f32), V((nc, high, width), f32), whole, whole, whole]
 
     D = pltpu.SemaphoreType.DMA
-    strip, band, both, left = pl.pallas_call(
+    operands = (an, un, uo, ln.T, lo.T, lot, uol, iln, iun, ilo, iuo)
+    results = pl.pallas_call(
         functools.partial(kernel, nr, nc, ny),
         out_shape=(
-            jax.ShapeDtypeStruct((wl, width), f32),
-            jax.ShapeDtypeStruct((width, cols), f32),
-            jax.ShapeDtypeStruct((nc, nr, 2 * width // nc // nr, width), f32),
-            jax.ShapeDtypeStruct((nc, nr, width // nc // nr, width), f32),
+            V((wl, width), f32),
+            V((width, cols), f32),
+            V((nc, nr, 2 * width // nc // nr, width), f32),
+            V((nc, nr, width // nc // nr, width), f32),
         ),
-        in_specs=[hbm, vm, vm, vm] + [hbm] * 6,
+        in_specs=[hbm] * 11,
         out_specs=(vm, vm, vm, vm),
         scratch_shapes=[
             V((rows, cols), f32), V((rows, cols), bf16), V((rows, cols), bf16),
-            V((2, nr, width // nr, wu), f32), V((nc, 2 * width // nc, wl), f32),
+            V((2, nr, width // nr, wu), f32), V((2, nc, width // nc, wl), f32),
             V((width, cols), f32), V((width, rows), f32),
             V((width, cols), f32), V((rows, width), f32),
             V((nz, ny, width, wu), f32), V((nz, width, wu), f32), V((nz, width, wu), f32),
             V((nc, wl, width), f32), V((width, wu), f32),
             V((width, wu), f32), V((width, wl), f32),
             *chain(2 * width), *chain(width),
-            V((6, width, width), f32), D, D((6,)), D((12, nr)), D((12, nr)), D((7, nc)), D((7, nc)),
+            V((6, width, width), f32), D, D((6,)), D((4,)), D((12, nr)), D((12, nr)), D((8, nc)), D((8, nc)),
         ],
-        compiler_params=pltpu.CompilerParams(collective_id=0, has_side_effects=True),
-    )(an, un, uo, l, lot, uol, iln, iun, ilo, iuo)
-    both = both.reshape(2 * width, width)
-    return both[width:], both[:width], strip, left.reshape(width, width), band
+        compiler_params=pltpu.CompilerParams(collective_id=0, has_side_effects=True, vmem_limit_bytes=LIMIT),
+    )(*[pltpu.with_memory_space_constraint(v, pltpu.HBM) for v in operands])
+    strip, band, both, left = results
+    shapes = [(width, width), (width, width), strip.shape, (width, width), band.shape]
+    return pl.pallas_call(
+        finish,
+        out_shape=[jax.ShapeDtypeStruct(shape, f32) for shape in shapes],
+        in_specs=[vm] * 4,
+        out_specs=[hbm] * 5,
+        scratch_shapes=[D((5,))],
+        compiler_params=pltpu.CompilerParams(vmem_limit_bytes=1 << 20),
+    )(strip, band, both.reshape(2 * width, width), left.reshape(width, width))
 
 
 def solution(mesh):

time: 88.2 us -> 82.3 us (0.933)
  the two profiles are of different devices: /device:TPU:0 before, /device:TPU:17 now
where the time goes in v1:
time: 82.3 us; the launch traced here: 82.2 us
  Pallas kernels  81.5 us (99%)
    pallas_call x1, Pallas kernels, body(): pl.pallas_call(functools.partial(kernel, nr, nc, ny), out_shape=(V((wl, w...  80.2 us

profile of v1, /device:TPU:17, one launch (start us, length us, event | category | flops | bytes accessed | tf_op | source)
XLA Modules:
  0.0 82.2 jit_solution(6174982163765067255)
XLA Ops:
  0.6 80.2 %shard_map.146 = (f32[128,256]{1,0:T(8,128)S(1)}, f32[256,1024]{1,0:T(8,128)S(1)}, f32[4,8,16,256]{3,2,1,0:T(8,128)S(1)}, f32[4,8,8,256]{3,2,1,0:T(8,128)S(1)}) custom-call(f32[512,1024]{1,0:T(8,128)} %a_hbm.1, f32[32,1024]{1,0:T(8,128)} %un_ref.1, f32[32,1024]{1,0:T(8,128)} %uo_ref.1, f32[64,512]{1,0:T(8,128)} %bitcast.6, f32[64,512]{1,0:T(8,128)} %bitcast.7, ...), custom_call_target="tpu_custom_call" | custom-call | tf_op jit(solution)/shard_map/pallas_call | solution.py:327
  80.9 1.3 %shard_map.147 = (f32[256,256]{1,0:T(8,128)}, f32[256,256]{1,0:T(8,128)}, f32[128,256]{1,0:T(8,128)}, f32[256,256]{1,0:T(8,128)}, f32[256,1024]{1,0:T(8,128)}) custom-call(f32[128,256]{1,0:T(8,128)S(1)} %get-tuple-element.9.strip_ref, f32[256,1024]{1,0:T(8,128)S(1)} %get-tuple-element.10.band_ref, f32[512,256]{1,0:T(8,128)S(1)} %bitcast.4, ...), custom_call_target="tpu_custom_call" | custom-call | tf_op jit(solution)/shard_map/pallas_call | solution.py:352

commit v2 on v1

v2 whole, which is shorter than its diff:
```python
import functools

import jax
import jax.numpy as jnp
from jax import lax
from jax.experimental import pallas as pl
from jax.experimental.pallas import tpu as pltpu
from jax.sharding import PartitionSpec as P

f32, bf16 = jnp.float32, jnp.bfloat16
NN, NT = ((1,), (0,)), ((1,), (1,))
LIMIT = 48 << 20


def split(x):
    high = x.astype(bf16)
    return high, (x - high.astype(f32)).astype(bf16)


def mul(a, b, dims=NN):
    def one(x, y):
        return lax.dot_general(x, y, (dims, ((), ())), preferred_element_type=f32)

    return one(a[0], b[0]) + (one(a[0], b[1]) + one(a[1], b[0]))


def flip(z, k):
    bit = 1
    while bit <= k:
        if k & bit:
            z = z + bit - 2 * bit * lax.rem(z // bit, 2)
        bit *= 2
    return z


def arrive(copies):
    for copy in copies:
        copy.wait_recv()


def kernel(
    nr, nc, ny, a_hbm, un_hbm, uo_hbm, ln_hbm, lo_hbm, lot_hbm, uol_hbm, iln_hbm, iun_hbm, ilo_hbm, iuo_hbm,
    strip_ref, band_ref, both_ref, top_ref,
    a_ref, ah, al, xu, xl, vh, vl, pb, ps, ry, sz, rz, rp, bc, gp, gr, gc,
    pt, rt, st, tt, gt, sq,
    asem, qsem, osem, rs_send, rs_recv, cs_send, cs_recv,
):
    r, c = lax.axis_index("row"), lax.axis_index("col")
    rows, cols = a_hbm.shape
    wl = rows // nc
    width = iln_hbm.shape[0]
    hu = width // nr
    nz = nr // ny
    z, y = r // ny, lax.rem(r, ny)
    even = nz & (nz - 1) == 0
    hops = list(range(1, nz))
    reach = lambda k: flip(z, k) if even else lax.rem(z + k, nz)
    origin = lambda k: flip(z, k) if even else lax.rem(z - k + nz, nz)
    cores = 2 if nc % 2 == 0 else 1
    nx = nc // cores
    x, core = c // cores, lax.rem(c, cores)

    load = pltpu.make_async_copy(a_hbm, a_ref, asem)
    squares = (iuo_hbm, uol_hbm, iun_hbm, iln_hbm, lot_hbm, ilo_hbm)
    loads = [pltpu.make_async_copy(m, sq.at[i], qsem.at[i]) for i, m in enumerate(squares)]
    own = [
        pltpu.make_async_copy(source, target, osem.at[i])
        for i, (source, target) in enumerate(
            [(un_hbm, xu.at[0, r]), (uo_hbm, xu.at[1, r]), (ln_hbm, xl.at[0, c]), (lo_hbm, xl.at[1, c])]
        )
    ]
    for copy in loads + own:
        copy.start()
    load.start()
    barrier = pltpu.get_barrier_semaphore()
    for d in range(1, nr):
        pl.semaphore_signal(barrier, inc=1, device_id={"row": lax.rem(r + d, nr)}, device_id_type=pl.DeviceIdType.MESH)
    for d in range(1, nc):
        pl.semaphore_signal(barrier, inc=1, device_id={"col": lax.rem(c + d, nc)}, device_id_type=pl.DeviceIdType.MESH)
    pl.semaphore_wait(barrier, nr + nc - 2)

    def lrow(i):
        return pl.ds(pl.multiple_of(i * wl, wl), wl)

    def urow(i):
        return pl.ds(pl.multiple_of(i * hu, hu), hu)

    sent = []

    def put(axis, peer, source, target, send, recv):
        copy = pltpu.make_async_remote_copy(
            src_ref=source,
            dst_ref=target,
            send_sem=send,
            recv_sem=recv,
            device_id={axis: peer},
            device_id_type=pl.DeviceIdType.MESH,
        )
        copy.start()
        sent.append(copy)
        return copy

    def push(stage, index, source, target, peer):
        return put("row", peer, source, target, rs_send.at[stage, index], rs_recv.at[stage, index])

    def toss(stage, index, source, target, peer):
        return put("col", peer, source, target, cs_send.at[stage, index], cs_recv.at[stage, index])

    def across(stage, k, source, slot):
        return [push(stage, k * ny + d, source, slot, z * ny + lax.rem(y + d, ny)) for d in range(1, ny)]

    def gather_start(stage, source, slot):
        over = across(stage + 1, 0, source, slot(r))
        along = {k: push(stage, k, source, slot(r), reach(k) * ny + y) for k in hops}
        return along, over

    def gather_pass(stage, state, slot, k):
        along, over = state
        along[k].wait_recv()
        here = slot(origin(k) * ny + y)
        over.extend(across(stage + 1, k, here, here))

    def twin(stage, k, source, target):
        if cores == 1:
            return []
        return [toss(stage, nx + k, source, target, x * cores + 1 - core)]

    def spread_start(stage, source, slot):
        along = [toss(stage, k, source, slot(c), lax.rem(x + k, nx) * cores + core) for k in range(1, nx)]
        return along, twin(stage, 0, source, slot(c))

    def spread_end(stage, state, slot):
        along, near = state
        for k in range(1, nx):
            along[k - 1].wait_recv()
            here = slot(lax.rem(x - k + nx, nx) * cores + core)
            near = near + twin(stage, k, here, here)
        return near

    def row_stage(stage, source, target):
        peers = [lax.rem(r + d, nr) for d in range(1, nr)]
        return [push(stage, d, source(p), target, p) for d, p in enumerate(peers, 1)]

    def col_stage(stage, source, target):
        peers = [lax.rem(c + d, nc) for d in range(1, nc)]
        return [toss(stage, d, source(p), target, p) for d, p in enumerate(peers, 1)]

    lslot = [lambda i: xl.at[0, i], lambda i: xl.at[1, i]]
    uslot = [lambda i: xu.at[0, i], lambda i: xu.at[1, i]]
    low = [spread_start(0, ln_hbm, lslot[0]), spread_start(1, lo_hbm, lslot[1])]
    up = [gather_start(0, un_hbm, uslot[0]), gather_start(2, uo_hbm, uslot[1])]
    for copy in own + loads:
        copy.wait()
    iuo, iun = split(sq[0]), split(sq[2])
    mix_u = split(mul(split(mul(iuo, split(sq[1]))), iun))
    ilo = sq[5]
    mix_l = mul(split(mul(split(sq[3]), split(sq[4]))), split(ilo))
    mix_l, ilo, iln = split(mix_l.T), split(ilo.T), split(sq[3].T)
    load.wait()
    high, rest = split(a_ref[...])
    ah[...] = high
    al[...] = rest
    gather_pass(0, up[0], uslot[0], hops[0])
    near = spread_end(0, low[0], lslot[0])
    near = near + spread_end(1, low[1], lslot[1])
    arrive(near)
    ln, lo = split(xl[0].reshape(width, rows)), split(xl[1].reshape(width, rows))
    lts = split(mul(ilo, lo) - mul(mix_l, ln))
    lns = split(mul(iln, ln))
    for i in range(cols // width):
        here = slice(i * width, (i + 1) * width)
        pb[:, here] = -mul(lts, (ah[:, here], al[:, here]))
    b0 = {}
    for k in hops[::-1] + [0]:
        zt = reach(k) if k else z
        peers = [zt * ny + lax.rem(y + d, ny) for d in range(1, ny)]
        b0[k] = [
            push(4, k * ny + d, pb.at[urow(p)], ry.at[k, d], z * ny + lax.rem(y + d, ny)) for d, p in enumerate(peers, 1)
        ]
    for k in hops[1:]:
        gather_pass(0, up[0], uslot[0], k)
    gather_pass(2, up[1], uslot[1], hops[0])
    b1 = {}
    for k in hops[::-1] + [0]:
        arrive(b0[k])
        zt = reach(k) if k else z
        total = pb[urow(zt * ny + y)]
        for d in range(1, ny):
            total = total + ry[k, d]
        if k:
            sz[k] = total
            b1[k] = push(5, k, sz.at[k], rz.at[k], zt * ny + y)
        else:
            rz[0] = total
    for k in hops[1:]:
        gather_pass(2, up[1], uslot[1], k)
    for state in up:
        arrive(state[1])
    for i in range(cols // width):
        here = slice(i * width, (i + 1) * width)
        un, uo = split(xu[0, :, :, here].reshape(width, width)), split(xu[1, :, :, here].reshape(width, width))
        vh[:width, here], vl[:width, here] = split(mul(iuo, uo) - mul(mix_u, un))
        vh[width:, here], vl[width:, here] = split(mul(iun, un))
    for i in range(rows // width):
        here = slice(i * width, (i + 1) * width)
        ps[here] = -mul((ah[here], al[here]), (vh[:width], vl[:width]), NT)
    pt[...] = -mul(lns, split(ps[...]))
    each = width // nc
    part = lambda p: pt.at[pl.ds(pl.multiple_of(p * each, each), each)]
    t0 = col_stage(3, part, rt.at[c])
    rt[c] = part(c)[...]
    p0 = col_stage(2, lambda p: ps.at[lrow(p)], rp.at[c])
    rp[c] = ps[lrow(c)]
    arrive([b1[k] for k in hops])
    band = rz[0]
    for k in hops:
        band = band + rz[k]
    bc[...] = band
    bslot = lambda i: band_ref.at[urow(i)]
    b2 = gather_start(6, bc, bslot)
    band_ref[urow(r)] = band
    gp[...] = -mul(split(band), (vh[...], vl[...]), NT)
    g0 = col_stage(4, lambda p: gp, gr.at[c])
    gr[c] = gp[...]
    arrive(t0)
    total = rt[0]
    for i in range(1, nc):
        total = total + rt[i]
    few = each // nr
    for i in range(nr):
        st[i] = total[i * few : (i + 1) * few]
    t1 = row_stage(10, lambda p: st.at[p], tt.at[r])
    tt[r] = st[r]
    gather_pass(6, b2, bslot, hops[0])
    arrive(g0)
    total = gr[0]
    for i in range(1, nc):
        total = total + gr[i]
    gc[...] = total
    cslot = lambda i: both_ref.at[urow(i)]
    g1 = gather_start(8, gc, cslot)
    both_ref[urow(r)] = total
    arrive(t1)
    total = tt[0]
    for i in range(1, nr):
        total = total + tt[i]
    gt[r] = total
    t2 = row_stage(11, lambda p: gt.at[r], gt.at[r])
    for k in hops[1:]:
        gather_pass(6, b2, bslot, k)
    arrive(p0)
    strip = rp[0]
    for i in range(1, nc):
        strip = strip + rp[i]
    strip_ref[...] = strip
    arrive(t2)
    tslot = lambda i: top_ref.at[i]
    t3 = spread_start(5, gt, tslot)
    top_ref[c] = gt[...]
    for k in hops:
        gather_pass(8, g1, cslot, k)
    arrive(spread_end(5, t3, tslot))
    arrive(b2[1])
    arrive(g1[1])
    for copy in sent:
        copy.wait_send()


def finish(strip_ref, band_ref, both_ref, top_ref, corner, top, bottom, left, right, sem):
    width = top_ref.shape[0]
    pairs = (
        (band_ref, right), (strip_ref, bottom), (top_ref, top),
        (both_ref.at[:, pl.ds(0, width)], corner), (both_ref.at[:, pl.ds(width, width)], left),
    )
    copies = [pltpu.make_async_copy(source, target, sem.at[i]) for i, (source, target) in enumerate(pairs)]
    for copy in copies:
        copy.start()
    for copy in copies:
        copy.wait()


def body(an, ln, un, lot, lo, uol, uo, dln, dun, iln, iun, dlo, duo, ilo, iuo):
    nr, nc = lax.axis_size("row"), lax.axis_size("col")
    rows, cols = an.shape
    width = iln.shape[0]
    hu, wl, each = width // nr, rows // nc, width // nc
    ny = nc // 2 if nc % 2 == 0 and nr % max(nc // 2, 1) == 0 else 1
    nz = nr // ny
    vm = pl.BlockSpec(memory_space=pltpu.VMEM)
    hbm = pl.BlockSpec(memory_space=pltpu.HBM)
    V, D = pltpu.VMEM, pltpu.SemaphoreType.DMA
    whole = V((nr, each // nr, width), f32)
    operands = (an, un, uo, ln.T, lo.T, lot, uol, iln, iun, ilo, iuo)
    strip, band, both, top = pl.pallas_call(
        functools.partial(kernel, nr, nc, ny),
        out_shape=(
            V((wl, width), f32), V((width, cols), f32), V((width, 2 * width), f32), V((nc, nr, each // nr, width), f32)
        ),
        in_specs=[hbm] * 11,
        out_specs=(vm, vm, vm, vm),
        scratch_shapes=[
            V((rows, cols), f32), V((rows, cols), bf16), V((rows, cols), bf16),
            V((2, nr, hu, cols), f32), V((2, nc, each, rows), f32),
            V((2 * width, cols), bf16), V((2 * width, cols), bf16),
            V((width, cols), f32), V((rows, width), f32),
            V((nz, ny, hu, cols), f32), V((nz, hu, cols), f32), V((nz, hu, cols), f32),
            V((nc, wl, width), f32), V((hu, cols), f32),
            V((hu, 2 * width), f32), V((nc, hu, 2 * width), f32), V((hu, 2 * width), f32),
            V((width, width), f32), V((nc, each, width), f32), whole, whole, whole,
            V((6, width, width), f32),
            D, D((6,)), D((4,)), D((12, nr)), D((12, nr)), D((6, nc)), D((6, nc)),
        ],
        compiler_params=pltpu.CompilerParams(collective_id=0, has_side_effects=True, vmem_limit_bytes=LIMIT),
    )(*[pltpu.with_memory_space_constraint(v, pltpu.HBM) for v in operands])
    shapes = [(width, width), (width, width), strip.shape, (width, width), band.shape]
    return pl.pallas_call(
        finish,
        out_shape=[jax.ShapeDtypeStruct(shape, f32) for shape in shapes],
        in_specs=[vm] * 4,
        out_specs=[hbm] * 5,
        scratch_shapes=[D((5,))],
        compiler_params=pltpu.CompilerParams(vmem_limit_bytes=1 << 20),
    )(strip, band, both, top.reshape(width, width))


def solution(mesh):
    two, whole = P("row", "col"), P()
    return jax.shard_map(
        body,
        mesh=mesh,
        in_specs=(two, two, two, whole, two, whole, two) + (whole,) * 8,
        out_specs=(P(), P(), P(("row", "col"), None), P(), P(None, "col")),
        check_vma=False,
    )
```

time: 82.3 us -> 77.5 us (0.942)
  the two profiles are of different devices: /device:TPU:17 before, /device:TPU:0 now
where the time goes in v2:
time: 77.5 us; the launch traced here: 77.4 us
  Pallas kernels  76.7 us (99%)
    pallas_call x1, Pallas kernels, body(): pl.pallas_call(functools.partial(kernel, nr, nc, ny), out_shape=(V((wl, w...  75.4 us

profile of v2, /device:TPU:0, one launch (start us, length us, event | category | flops | bytes accessed | tf_op | source)
XLA Modules:
  0.0 77.4 jit_solution(10865365559286620753)
XLA Ops:
  0.6 75.4 %shard_map.146 = (f32[128,256]{1,0:T(8,128)S(1)}, f32[256,1024]{1,0:T(8,128)S(1)}, f32[256,512]{1,0:T(8,128)S(1)}, f32[4,8,8,256]{3,2,1,0:T(8,128)S(1)}) custom-call(f32[512,1024]{1,0:T(8,128)} %a_hbm.1, f32[32,1024]{1,0:T(8,128)} %un_hbm.1, f32[32,1024]{1,0:T(8,128)} %uo_hbm.1, f32[64,512]{1,0:T(8,128)} %bitcast.4, f32[64,512]{1,0:T(8,128)} %bitcast.5, ...), custom_call_target="tpu_custom_call" | custom-call | tf_op jit(solution)/shard_map/pallas_call | solution.py:294
  76.1 1.3 %shard_map.147 = (f32[256,256]{1,0:T(8,128)}, f32[256,256]{1,0:T(8,128)}, f32[128,256]{1,0:T(8,128)}, f32[256,256]{1,0:T(8,128)}, f32[256,1024]{1,0:T(8,128)}) custom-call(f32[128,256]{1,0:T(8,128)S(1)} %get-tuple-element.9.strip_ref, f32[256,1024]{1,0:T(8,128)S(1)} %get-tuple-element.10.band_ref, f32[256,512]{1,0:T(8,128)S(1)} %get-tuple-element.11.both_ref, ...), custom_call_target="tpu_custom_call" | custom-call | tf_op jit(solution)/shard_map/pallas_call | solution.py:316

commit v3 on v2

--- a/solution.py
+++ b/solution.py
@@ -106,19 +106,63 @@
     def toss(stage, index, source, target, peer):
         return put("col", peer, source, target, cs_send.at[stage, index], cs_recv.at[stage, index])
 
-    def across(stage, k, source, slot):
-        return [push(stage, k * ny + d, source, slot, z * ny + lax.rem(y + d, ny)) for d in range(1, ny)]
-
-    def gather_start(stage, source, slot):
-        over = across(stage + 1, 0, source, slot(r))
-        along = {k: push(stage, k, source, slot(r), reach(k) * ny + y) for k in hops}
-        return along, over
-
-    def gather_pass(stage, state, slot, k):
-        along, over = state
-        along[k].wait_recv()
-        here = slot(origin(k) * ny + y)
-        over.extend(across(stage + 1, k, here, here))
+    quad = nz == 4
+
+    def across(stage, k, zk, slot, source=None):
+        here = slot(zk * ny + y)
+        base = 3 + 2 * ny + k * ny
+        source = here if source is None else source
+        return [push(stage, base + d, source, here, z * ny + lax.rem(y + d, ny)) for d in range(1, ny)]
+
+    def gather(stage, source, slot, flat):
+        here = slot(r)
+        near = lambda i, chunk, origin=None: push(
+            stage, i, slot(chunk) if origin is None else origin, slot(chunk), flip(z, 1) * ny + y
+        )
+        over = across(stage, 0, z, slot, source)
+        if not quad:
+            along = [push(stage, k, source, here, reach(k) * ny + y) for k in hops]
+
+            def relay(k):
+                def step():
+                    along[k - 1].wait_recv()
+                    over.extend(across(stage, k, origin(k), slot))
+
+                return step
+
+            steps = [relay(k) for k in hops]
+            return steps + [lambda: None] * (3 - len(steps)) + [lambda: arrive(over)]
+        far = push(stage, 1, source, here, flip(z, 2) * ny + y)
+        first = near(0, r, source)
+        ends, mid = [], []
+
+        def one():
+            if flat:
+                arrive(over)
+                for d in range(1, ny):
+                    ends.append(near(2 + d, z * ny + lax.rem(y - d + ny, ny)))
+            else:
+                first.wait_recv()
+                over.extend(across(stage, 1, flip(z, 1), slot))
+
+        def two():
+            far.wait_recv()
+            mid.append(near(2, flip(z, 2) * ny + y))
+            (ends if flat else over).extend(across(stage, 2, flip(z, 2), slot))
+
+        def three():
+            if flat:
+                arrive(ends[ny - 1 :])
+                for d in range(1, ny):
+                    mid.append(near(2 + ny + d, flip(z, 2) * ny + lax.rem(y - d + ny, ny)))
+            else:
+                arrive(mid)
+                over.extend(across(stage, 3, flip(z, 3), slot))
+
+        def four():
+            arrive([first] + ends[: ny - 1] + mid if flat else over)
+
+        return [one, two, three, four]
 
     def twin(stage, k, source, target):
         if cores == 1:
@@ -148,7 +192,7 @@
     lslot = [lambda i: xl.at[0, i], lambda i: xl.at[1, i]]
     uslot = [lambda i: xu.at[0, i], lambda i: xu.at[1, i]]
     low = [spread_start(0, ln_hbm, lslot[0]), spread_start(1, lo_hbm, lslot[1])]
-    up = [gather_start(0, un_hbm, uslot[0]), gather_start(2, uo_hbm, uslot[1])]
+    up = [gather(0, un_hbm, uslot[0], False), gather(1, uo_hbm, uslot[1], True)]
     for copy in own + loads:
         copy.wait()
     iuo, iun = split(sq[0]), split(sq[2])
@@ -160,7 +204,9 @@
     high, rest = split(a_ref[...])
     ah[...] = high
     al[...] = rest
-    gather_pass(0, up[0], uslot[0], hops[0])
+    up[0][0]()
+    up[1][0]()
+    up[0][1]()
     near = spread_end(0, low[0], lslot[0])
     near = near + spread_end(1, low[1], lslot[1])
     arrive(near)
@@ -177,9 +223,8 @@
         b0[k] = [
             push(4, k * ny + d, pb.at[urow(p)], ry.at[k, d], z * ny + lax.rem(y + d, ny)) for d, p in enumerate(peers, 1)
         ]
-    for k in hops[1:]:
-        gather_pass(0, up[0], uslot[0], k)
-    gather_pass(2, up[1], uslot[1], hops[0])
+    up[1][1]()
+    up[0][2]()
     b1 = {}
     for k in hops[::-1] + [0]:
         arrive(b0[k])
@@ -192,10 +237,9 @@
             b1[k] = push(5, k, sz.at[k], rz.at[k], zt * ny + y)
         else:
             rz[0] = total
-    for k in hops[1:]:
-        gather_pass(2, up[1], uslot[1], k)
-    for state in up:
-        arrive(state[1])
+    up[1][2]()
+    up[0][3]()
+    up[1][3]()
     for i in range(cols // width):
         here = slice(i * width, (i + 1) * width)
         un, uo = split(xu[0, :, :, here].reshape(width, width)), split(xu[1, :, :, here].reshape(width, width))
@@ -217,7 +261,7 @@
         band = band + rz[k]
     bc[...] = band
     bslot = lambda i: band_ref.at[urow(i)]
-    b2 = gather_start(6, bc, bslot)
+    b2 = gather(2, bc, bslot, False)
     band_ref[urow(r)] = band
     gp[...] = -mul(split(band), (vh[...], vl[...]), NT)
     g0 = col_stage(4, lambda p: gp, gr.at[c])
@@ -229,25 +273,27 @@
     few = each // nr
     for i in range(nr):
         st[i] = total[i * few : (i + 1) * few]
-    t1 = row_stage(10, lambda p: st.at[p], tt.at[r])
+    t1 = row_stage(6, lambda p: st.at[p], tt.at[r])
     tt[r] = st[r]
-    gather_pass(6, b2, bslot, hops[0])
+    b2[0]()
+    b2[1]()
     arrive(g0)
     total = gr[0]
     for i in range(1, nc):
         total = total + gr[i]
     gc[...] = total
     cslot = lambda i: both_ref.at[urow(i)]
-    g1 = gather_start(8, gc, cslot)
+    g1 = gather(3, gc, cslot, True)
     both_ref[urow(r)] = total
     arrive(t1)
     total = tt[0]
     for i in range(1, nr):
         total = total + tt[i]
     gt[r] = total
-    t2 = row_stage(11, lambda p: gt.at[r], gt.at[r])
-    for k in hops[1:]:
-        gather_pass(6, b2, bslot, k)
+    t2 = row_stage(7, lambda p: gt.at[r], gt.at[r])
+    b2[2]()
+    g1[0]()
+    g1[1]()
     arrive(p0)
     strip = rp[0]
     for i in range(1, nc):
@@ -257,11 +303,10 @@
     tslot = lambda i: top_ref.at[i]
     t3 = spread_start(5, gt, tslot)
     top_ref[c] = gt[...]
-    for k in hops:
-        gather_pass(8, g1, cslot, k)
+    g1[2]()
     arrive(spread_end(5, t3, tslot))
-    arrive(b2[1])
-    arrive(g1[1])
+    b2[3]()
+    g1[3]()
     for copy in sent:
         copy.wait_send()
 
@@ -289,6 +334,7 @@
     vm = pl.BlockSpec(memory_space=pltpu.VMEM)
     hbm = pl.BlockSpec(memory_space=pltpu.HBM)
     V, D = pltpu.VMEM, pltpu.SemaphoreType.DMA
+    lanes = max(nr, 3 + (2 + nz) * ny)
     whole = V((nr, each // nr, width), f32)
     operands = (an, un, uo, ln.T, lo.T, lot, uol, iln, iun, ilo, iuo)
     strip, band, both, top = pl.pallas_call(
@@ -308,7 +354,7 @@
             V((hu, 2 * width), f32), V((nc, hu, 2 * width), f32), V((hu, 2 * width), f32),
             V((width, width), f32), V((nc, each, width), f32), whole, whole, whole,
             V((6, width, width), f32),
-            D, D((6,)), D((4,)), D((12, nr)), D((12, nr)), D((6, nc)), D((6, nc)),
+            D, D((6,)), D((4,)), D((8, lanes)), D((8, lanes)), D((6, nc)), D((6, nc)),
         ],
         compiler_params=pltpu.CompilerParams(collective_id=0, has_side_effects=True, vmem_limit_bytes=LIMIT),
     )(*[pltpu.with_memory_space_constraint(v, pltpu.HBM) for v in operands])

time: 77.5 us -> 72.5 us (0.935)
  Pallas kernels: 76.7 us -> 71.7 us
    pallas_call x1, Pallas kernels: 75.4 us -> 70.4 us  [body(): pl.pallas_call(functools.partial(kernel, nr, nc, ny), out_shape=(V((wl, w...]
where the time goes in v3:
time: 72.5 us; the launch traced here: 72.4 us
  Pallas kernels  71.7 us (99%)
    pallas_call x1, Pallas kernels, body(): pl.pallas_call(functools.partial(kernel, nr, nc, ny), out_shape=(V((wl, w...  70.4 us

profile of v3, /device:TPU:0, one launch (start us, length us, event | category | flops | bytes accessed | tf_op | source)
XLA Modules:
  0.0 72.4 jit_solution(10489525599890274418)
XLA Ops:
  0.6 70.4 %shard_map.146 = (f32[128,256]{1,0:T(8,128)S(1)}, f32[256,1024]{1,0:T(8,128)S(1)}, f32[256,512]{1,0:T(8,128)S(1)}, f32[4,8,8,256]{3,2,1,0:T(8,128)S(1)}) custom-call(f32[512,1024]{1,0:T(8,128)} %a_hbm.1, f32[32,1024]{1,0:T(8,128)} %un_hbm.1, f32[32,1024]{1,0:T(8,128)} %uo_hbm.1, f32[64,512]{1,0:T(8,128)} %bitcast.4, f32[64,512]{1,0:T(8,128)} %bitcast.5, ...), custom_call_target="tpu_custom_call" | custom-call | tf_op jit(solution)/shard_map/pallas_call | solution.py:340
  71.1 1.3 %shard_map.147 = (f32[256,256]{1,0:T(8,128)}, f32[256,256]{1,0:T(8,128)}, f32[128,256]{1,0:T(8,128)}, f32[256,256]{1,0:T(8,128)}, f32[256,1024]{1,0:T(8,128)}) custom-call(f32[128,256]{1,0:T(8,128)S(1)} %get-tuple-element.9.strip_ref, f32[256,1024]{1,0:T(8,128)S(1)} %get-tuple-element.10.band_ref, f32[256,512]{1,0:T(8,128)S(1)} %get-tuple-element.11.both_ref, ...), custom_call_target="tpu_custom_call" | custom-call | tf_op jit(solution)/shard_map/pallas_call | solution.py:362

commit v4 on v3

--- a/solution.py
+++ b/solution.py
@@ -41,8 +41,8 @@
 def kernel(
     nr, nc, ny, a_hbm, un_hbm, uo_hbm, ln_hbm, lo_hbm, lot_hbm, uol_hbm, iln_hbm, iun_hbm, ilo_hbm, iuo_hbm,
     strip_ref, band_ref, both_ref, top_ref,
-    a_ref, ah, al, xu, xl, vh, vl, pb, ps, ry, sz, rz, rp, bc, gp, gr, gc,
-    pt, rt, st, tt, gt, sq,
+    a_ref, ah, al, xu, xl, vh, vl, pb, ps, ry, sz, rz, fp, tp, rp, bc, gp, gn, gr, gc,
+    pt, nt, ft, rt, st, tt, gt, sq,
     asem, qsem, osem, rs_send, rs_recv, cs_send, cs_recv,
 ):
     r, c = lax.axis_index("row"), lax.axis_index("col")
@@ -56,7 +56,7 @@
     hops = list(range(1, nz))
     reach = lambda k: flip(z, k) if even else lax.rem(z + k, nz)
     origin = lambda k: flip(z, k) if even else lax.rem(z - k + nz, nz)
-    cores = 2 if nc % 2 == 0 else 1
+    cores = 2
     nx = nc // cores
     x, core = c // cores, lax.rem(c, cores)
 
@@ -164,10 +164,10 @@
 
         return [one, two, three, four]
 
+    other = x * cores + 1 - core
+
     def twin(stage, k, source, target):
-        if cores == 1:
-            return []
-        return [toss(stage, nx + k, source, target, x * cores + 1 - core)]
+        return [toss(stage, nx + k, source, target, other)]
 
     def spread_start(stage, source, slot):
         along = [toss(stage, k, source, slot(c), lax.rem(x + k, nx) * cores + core) for k in range(1, nx)]
@@ -185,9 +185,28 @@
         peers = [lax.rem(r + d, nr) for d in range(1, nr)]
         return [push(stage, d, source(p), target, p) for d, p in enumerate(peers, 1)]
 
-    def col_stage(stage, source, target):
-        peers = [lax.rem(c + d, nc) for d in range(1, nc)]
-        return [toss(stage, d, source(p), target, p) for d, p in enumerate(peers, 1)]
+    def fold_near(stage, block, got):
+        return [toss(stage, q, block(q * cores + 1 - core), got.at[q], other) for q in range(nx)]
+
+    def fold_far(stage, copies, block, near, send, got):
+        arrive(copies)
+        out = []
+        for k in [*range(1, nx), 0]:
+            q = lax.rem(x + k, nx)
+            total = block(q * cores + core)[...] + near[q]
+            if k:
+                send[k] = total
+                out.append(toss(stage, nx + k, send.at[k], got.at[k], q * cores + core))
+            else:
+                got[0] = total
+        return out
+
+    def fold_end(copies, got):
+        arrive(copies)
+        total = got[0]
+        for k in range(1, nx):
+            total = total + got[k]
+        return total
 
     lslot = [lambda i: xl.at[0, i], lambda i: xl.at[1, i]]
     uslot = [lambda i: xu.at[0, i], lambda i: xu.at[1, i]]
@@ -216,6 +235,8 @@
     for i in range(cols // width):
         here = slice(i * width, (i + 1) * width)
         pb[:, here] = -mul(lts, (ah[:, here], al[:, here]))
+    up[1][1]()
+    up[0][2]()
     b0 = {}
     for k in hops[::-1] + [0]:
         zt = reach(k) if k else z
@@ -223,8 +244,6 @@
         b0[k] = [
             push(4, k * ny + d, pb.at[urow(p)], ry.at[k, d], z * ny + lax.rem(y + d, ny)) for d, p in enumerate(peers, 1)
         ]
-    up[1][1]()
-    up[0][2]()
     b1 = {}
     for k in hops[::-1] + [0]:
         arrive(b0[k])
@@ -237,7 +256,8 @@
             b1[k] = push(5, k, sz.at[k], rz.at[k], zt * ny + y)
         else:
             rz[0] = total
-    up[1][2]()
+        if k == hops[-1]:
+            up[1][2]()
     up[0][3]()
     up[1][3]()
     for i in range(cols // width):
@@ -251,10 +271,9 @@
     pt[...] = -mul(lns, split(ps[...]))
     each = width // nc
     part = lambda p: pt.at[pl.ds(pl.multiple_of(p * each, each), each)]
-    t0 = col_stage(3, part, rt.at[c])
-    rt[c] = part(c)[...]
-    p0 = col_stage(2, lambda p: ps.at[lrow(p)], rp.at[c])
-    rp[c] = ps[lrow(c)]
+    piece = lambda p: ps.at[lrow(p)]
+    t0 = fold_near(3, part, nt)
+    t0 = fold_far(3, t0, part, nt, ft, rt)
     arrive([b1[k] for k in hops])
     band = rz[0]
     for k in hops:
@@ -264,12 +283,15 @@
     b2 = gather(2, bc, bslot, False)
     band_ref[urow(r)] = band
     gp[...] = -mul(split(band), (vh[...], vl[...]), NT)
-    g0 = col_stage(4, lambda p: gp, gr.at[c])
-    gr[c] = gp[...]
-    arrive(t0)
-    total = rt[0]
-    for i in range(1, nc):
-        total = total + rt[i]
+    half = lambda i: gp.at[:, pl.ds(pl.multiple_of(i * width, width), width)]
+    g0 = [toss(4, 0, half(1 - core), gn, other)]
+    p0 = fold_near(2, piece, fp)
+    arrive(g0)
+    mine = half(core)[...] + gn[...]
+    gr[0] = mine
+    g0 = [toss(4, k, gr.at[0], gr.at[k], lax.rem(x + k, nx) * cores + core) for k in range(1, nx)]
+    p0 = fold_far(2, p0, piece, fp, tp, rp)
+    total = fold_end(t0, rt)
     few = each // nr
     for i in range(nr):
         st[i] = total[i * few : (i + 1) * few]
@@ -277,14 +299,11 @@
     tt[r] = st[r]
     b2[0]()
     b2[1]()
-    arrive(g0)
-    total = gr[0]
-    for i in range(1, nc):
-        total = total + gr[i]
+    total = fold_end(g0, gr)
     gc[...] = total
-    cslot = lambda i: both_ref.at[urow(i)]
+    cslot = lambda i: both_ref.at[core, urow(i)]
     g1 = gather(3, gc, cslot, True)
-    both_ref[urow(r)] = total
+    both_ref[core, urow(r)] = total
     arrive(t1)
     total = tt[0]
     for i in range(1, nr):
@@ -294,28 +313,26 @@
     b2[2]()
     g1[0]()
     g1[1]()
-    arrive(p0)
-    strip = rp[0]
-    for i in range(1, nc):
-        strip = strip + rp[i]
-    strip_ref[...] = strip
+    strip_ref[...] = fold_end(p0, rp)
     arrive(t2)
     tslot = lambda i: top_ref.at[i]
     t3 = spread_start(5, gt, tslot)
     top_ref[c] = gt[...]
     g1[2]()
-    arrive(spread_end(5, t3, tslot))
+    g1[3]()
+    g2 = toss(4, nx, both_ref.at[core], both_ref.at[core], other)
+    t3 = spread_end(5, t3, tslot)
     b2[3]()
-    g1[3]()
+    arrive(t3)
+    arrive([g2])
     for copy in sent:
         copy.wait_send()
 
 
 def finish(strip_ref, band_ref, both_ref, top_ref, corner, top, bottom, left, right, sem):
-    width = top_ref.shape[0]
     pairs = (
         (band_ref, right), (strip_ref, bottom), (top_ref, top),
-        (both_ref.at[:, pl.ds(0, width)], corner), (both_ref.at[:, pl.ds(width, width)], left),
+        (both_ref.at[0], corner), (both_ref.at[1], left),
     )
     copies = [pltpu.make_async_copy(source, target, sem.at[i]) for i, (source, target) in enumerate(pairs)]
     for copy in copies:
@@ -329,7 +346,7 @@
     rows, cols = an.shape
     width = iln.shape[0]
     hu, wl, each = width // nr, rows // nc, width // nc
-    ny = nc // 2 if nc % 2 == 0 and nr % max(nc // 2, 1) == 0 else 1
+    ny = nc // 2 if nr % (nc // 2) == 0 else 1
     nz = nr // ny
     vm = pl.BlockSpec(memory_space=pltpu.VMEM)
     hbm = pl.BlockSpec(memory_space=pltpu.HBM)
@@ -340,7 +357,7 @@
     strip, band, both, top = pl.pallas_call(
         functools.partial(kernel, nr, nc, ny),
         out_shape=(
-            V((wl, width), f32), V((width, cols), f32), V((width, 2 * width), f32), V((nc, nr, each // nr, width), f32)
+            V((wl, width), f32), V((width, cols), f32), V((2, width, width), f32), V((nc, nr, each // nr, width), f32)
         ),
         in_specs=[hbm] * 11,
         out_specs=(vm, vm, vm, vm),
@@ -350,9 +367,9 @@
             V((2 * width, cols), bf16), V((2 * width, cols), bf16),
             V((width, cols), f32), V((rows, width), f32),
             V((nz, ny, hu, cols), f32), V((nz, hu, cols), f32), V((nz, hu, cols), f32),
-            V((nc, wl, width), f32), V((hu, cols), f32),
-            V((hu, 2 * width), f32), V((nc, hu, 2 * width), f32), V((hu, 2 * width), f32),
-            V((width, width), f32), V((nc, each, width), f32), whole, whole, whole,
+            *[V((nc // 2, wl, width), f32)] * 3, V((hu, cols), f32),
+            V((hu, 2 * width), f32), V((hu, width), f32), V((nc // 2, hu, width), f32), V((hu, width), f32),
+            V((width, width), f32), *[V((nc // 2, each, width), f32)] * 3, whole, whole, whole,
             V((6, width, width), f32),
             D, D((6,)), D((4,)), D((8, lanes)), D((8, lanes)), D((6, nc)), D((6, nc)),
         ],

time: 72.5 us -> 75.3 us (1.039)
  Pallas kernels: 71.7 us -> 74.5 us
    pallas_call x1, Pallas kernels: 70.4 us -> 73.2 us  [body(): pl.pallas_call(functools.partial(kernel, nr, nc, ny), out_shape=(V((wl, w...]
where the time goes in v4:
time: 75.3 us; the launch traced here: 75.2 us
  Pallas kernels  74.5 us (99%)
    pallas_call x1, Pallas kernels, body(): pl.pallas_call(functools.partial(kernel, nr, nc, ny), out_shape=(V((wl, w...  73.2 us

profile of v4, /device:TPU:0, one launch (start us, length us, event | category | flops | bytes accessed | tf_op | source)
XLA Modules:
  0.0 75.2 jit_solution(18186443537634579238)
XLA Ops:
  0.6 73.2 %shard_map.146 = (f32[128,256]{1,0:T(8,128)S(1)}, f32[256,1024]{1,0:T(8,128)S(1)}, f32[2,256,256]{2,1,0:T(8,128)S(1)}, f32[4,8,8,256]{3,2,1,0:T(8,128)S(1)}) custom-call(f32[512,1024]{1,0:T(8,128)} %a_hbm.1, f32[32,1024]{1,0:T(8,128)} %un_hbm.1, f32[32,1024]{1,0:T(8,128)} %uo_hbm.1, f32[64,512]{1,0:T(8,128)} %bitcast.4, f32[64,512]{1,0:T(8,128)} %bitcast.5, ...), custom_call_target="tpu_custom_call" | custom-call | tf_op jit(solution)/shard_map/pallas_call | solution.py:357
  73.9 1.3 %shard_map.147 = (f32[256,256]{1,0:T(8,128)}, f32[256,256]{1,0:T(8,128)}, f32[128,256]{1,0:T(8,128)}, f32[256,256]{1,0:T(8,128)}, f32[256,1024]{1,0:T(8,128)}) custom-call(f32[128,256]{1,0:T(8,128)S(1)} %get-tuple-element.9.strip_ref, f32[256,1024]{1,0:T(8,128)S(1)} %get-tuple-element.10.band_ref, f32[2,256,256]{2,1,0:T(8,128)S(1)} %get-tuple-element.11.both_ref, ...), custom_call_target="tpu_custom_call" | custom-call | tf_op jit(solution)/shard_map/pallas_call | solution.py:379

commit v5 on v4

--- a/solution.py
+++ b/solution.py
@@ -235,8 +235,6 @@
     for i in range(cols // width):
         here = slice(i * width, (i + 1) * width)
         pb[:, here] = -mul(lts, (ah[:, here], al[:, here]))
-    up[1][1]()
-    up[0][2]()
     b0 = {}
     for k in hops[::-1] + [0]:
         zt = reach(k) if k else z
@@ -244,6 +242,8 @@
         b0[k] = [
             push(4, k * ny + d, pb.at[urow(p)], ry.at[k, d], z * ny + lax.rem(y + d, ny)) for d, p in enumerate(peers, 1)
         ]
+    up[1][1]()
+    up[0][2]()
     b1 = {}
     for k in hops[::-1] + [0]:
         arrive(b0[k])
@@ -297,28 +297,28 @@
         st[i] = total[i * few : (i + 1) * few]
     t1 = row_stage(6, lambda p: st.at[p], tt.at[r])
     tt[r] = st[r]
-    b2[0]()
-    b2[1]()
     total = fold_end(g0, gr)
     gc[...] = total
     cslot = lambda i: both_ref.at[core, urow(i)]
     g1 = gather(3, gc, cslot, True)
     both_ref[core, urow(r)] = total
+    b2[0]()
+    b2[1]()
     arrive(t1)
     total = tt[0]
     for i in range(1, nr):
         total = total + tt[i]
     gt[r] = total
     t2 = row_stage(7, lambda p: gt.at[r], gt.at[r])
-    b2[2]()
     g1[0]()
     g1[1]()
+    b2[2]()
+    g1[2]()
     strip_ref[...] = fold_end(p0, rp)
     arrive(t2)
     tslot = lambda i: top_ref.at[i]
     t3 = spread_start(5, gt, tslot)
     top_ref[c] = gt[...]
-    g1[2]()
     g1[3]()
     g2 = toss(4, nx, both_ref.at[core], both_ref.at[core], other)
     t3 = spread_end(5, t3, tslot)

time: 75.3 us -> 71.3 us (0.947)
  Pallas kernels: 74.5 us -> 70.5 us
    pallas_call x1, Pallas kernels: 73.2 us -> 69.2 us  [body(): pl.pallas_call(functools.partial(kernel, nr, nc, ny), out_shape=(V((wl, w...]
where the time goes in v5:
time: 71.3 us; the launch traced here: 71.1 us
  Pallas kernels  70.5 us (99%)
    pallas_call x1, Pallas kernels, body(): pl.pallas_call(functools.partial(kernel, nr, nc, ny), out_shape=(V((wl, w...  69.2 us

profile of v5, /device:TPU:0, one launch (start us, length us, event | category | flops | bytes accessed | tf_op | source)
XLA Modules:
  0.0 71.1 jit_solution(2300538847047829738)
XLA Ops:
  0.6 69.2 %shard_map.146 = (f32[128,256]{1,0:T(8,128)S(1)}, f32[256,1024]{1,0:T(8,128)S(1)}, f32[2,256,256]{2,1,0:T(8,128)S(1)}, f32[4,8,8,256]{3,2,1,0:T(8,128)S(1)}) custom-call(f32[512,1024]{1,0:T(8,128)} %a_hbm.1, f32[32,1024]{1,0:T(8,128)} %un_hbm.1, f32[32,1024]{1,0:T(8,128)} %uo_hbm.1, f32[64,512]{1,0:T(8,128)} %bitcast.4, f32[64,512]{1,0:T(8,128)} %bitcast.5, ...), custom_call_target="tpu_custom_call" | custom-call | tf_op jit(solution)/shard_map/pallas_call | solution.py:357
  69.8 1.3 %shard_map.147 = (f32[256,256]{1,0:T(8,128)}, f32[256,256]{1,0:T(8,128)}, f32[128,256]{1,0:T(8,128)}, f32[256,256]{1,0:T(8,128)}, f32[256,1024]{1,0:T(8,128)}) custom-call(f32[128,256]{1,0:T(8,128)S(1)} %get-tuple-element.9.strip_ref, f32[256,1024]{1,0:T(8,128)S(1)} %get-tuple-element.10.band_ref, f32[2,256,256]{2,1,0:T(8,128)S(1)} %get-tuple-element.11.both_ref, ...), custom_call_target="tpu_custom_call" | custom-call | tf_op jit(solution)/shard_map/pallas_call | solution.py:379

commit v6 on v5

--- a/solution.py
+++ b/solution.py
@@ -42,8 +42,8 @@
     nr, nc, ny, a_hbm, un_hbm, uo_hbm, ln_hbm, lo_hbm, lot_hbm, uol_hbm, iln_hbm, iun_hbm, ilo_hbm, iuo_hbm,
     strip_ref, band_ref, both_ref, top_ref,
     a_ref, ah, al, xu, xl, vh, vl, pb, ps, ry, sz, rz, fp, tp, rp, bc, gp, gn, gr, gc,
-    pt, nt, ft, rt, st, tt, gt, sq,
-    asem, qsem, osem, rs_send, rs_recv, cs_send, cs_recv,
+    pt, nt, st, tt, sq,
+    asem, qsem, osem, rs_send, rs_recv, cs_send, cs_recv, ws_send, ws_recv,
 ):
     r, c = lax.axis_index("row"), lax.axis_index("col")
     rows, cols = a_hbm.shape
@@ -93,7 +93,7 @@
             dst_ref=target,
             send_sem=send,
             recv_sem=recv,
-            device_id={axis: peer},
+            device_id=peer if axis is None else {axis: peer},
             device_id_type=pl.DeviceIdType.MESH,
         )
         copy.start()
@@ -223,29 +223,33 @@
     high, rest = split(a_ref[...])
     ah[...] = high
     al[...] = rest
-    up[0][0]()
-    up[1][0]()
-    up[0][1]()
-    near = spread_end(0, low[0], lslot[0])
-    near = near + spread_end(1, low[1], lslot[1])
-    arrive(near)
-    ln, lo = split(xl[0].reshape(width, rows)), split(xl[1].reshape(width, rows))
-    lts = split(mul(ilo, lo) - mul(mix_l, ln))
-    lns = split(mul(iln, ln))
-    for i in range(cols // width):
-        here = slice(i * width, (i + 1) * width)
-        pb[:, here] = -mul(lts, (ah[:, here], al[:, here]))
-    b0 = {}
-    for k in hops[::-1] + [0]:
+    q = {}
+    b0, b1 = {}, {}
+    each, few = width // nc, width // nc // nr
+    part = lambda p: pt.at[pl.ds(pl.multiple_of(p * each, each), each)]
+    piece = lambda p: ps.at[lrow(p)]
+    half = lambda i: gp.at[:, pl.ds(pl.multiple_of(i * width, width), width)]
+    cslot = lambda i: both_ref.at[core, urow(i)]
+
+    def lower():
+        near = spread_end(0, low[0], lslot[0])
+        near = near + spread_end(1, low[1], lslot[1])
+        arrive(near)
+        ln, lo = split(xl[0].reshape(width, rows)), split(xl[1].reshape(width, rows))
+        lts = split(mul(ilo, lo) - mul(mix_l, ln))
+        q["lns"] = split(mul(iln, ln))
+        for i in range(cols // width):
+            here = slice(i * width, (i + 1) * width)
+            pb[:, here] = -mul(lts, (ah[:, here], al[:, here]))
+
+    def spill(k):
         zt = reach(k) if k else z
         peers = [zt * ny + lax.rem(y + d, ny) for d in range(1, ny)]
         b0[k] = [
             push(4, k * ny + d, pb.at[urow(p)], ry.at[k, d], z * ny + lax.rem(y + d, ny)) for d, p in enumerate(peers, 1)
         ]
-    up[1][1]()
-    up[0][2]()
-    b1 = {}
-    for k in hops[::-1] + [0]:
+
+    def pile(k):
         arrive(b0[k])
         zt = reach(k) if k else z
         total = pb[urow(zt * ny + y)]
@@ -256,75 +260,118 @@
             b1[k] = push(5, k, sz.at[k], rz.at[k], zt * ny + y)
         else:
             rz[0] = total
-        if k == hops[-1]:
-            up[1][2]()
+
+    def upper():
+        for i in range(cols // width):
+            here = slice(i * width, (i + 1) * width)
+            un, uo = split(xu[0, :, :, here].reshape(width, width)), split(xu[1, :, :, here].reshape(width, width))
+            vh[:width, here], vl[:width, here] = split(mul(iuo, uo) - mul(mix_u, un))
+            vh[width:, here], vl[width:, here] = split(mul(iun, un))
+        for i in range(rows // width):
+            here = slice(i * width, (i + 1) * width)
+            ps[here] = -mul((ah[here], al[here]), (vh[:width], vl[:width]), NT)
+        pt[...] = -mul(q["lns"], split(ps[...]))
+        q["t0"] = fold_near(3, part, nt)
+
+    def wide(stage, source, target):
+        out = []
+        for n in range(1, nx * nr):
+            qx, p = lax.rem(x + n // nr, nx), lax.rem(r + n % nr, nr)
+            peer = {"row": p, "col": qx * cores + core}
+            out.append(put(None, peer, source(qx, p), target, ws_send.at[stage, n], ws_recv.at[stage, n]))
+        return out
+
+    def top_far():
+        arrive(q["t0"])
+        for i in range(nx):
+            total = part(i * cores + core)[...] + nt[i]
+            for k in range(nr):
+                st[i, k] = total[k * few : (k + 1) * few]
+        q["t1"] = wide(0, lambda i, p: st.at[i, p], tt.at[x, r])
+        tt[x, r] = st[x, r]
+
+    def band():
+        arrive([b1[k] for k in hops])
+        total = rz[0]
+        for k in hops:
+            total = total + rz[k]
+        bc[...] = total
+        band_ref[urow(r)] = total
+        q["b"] = gather(2, bc, lambda i: band_ref.at[urow(i)], False)
+
+    def inner():
+        gp[...] = -mul(split(bc[...]), (vh[...], vl[...]), NT)
+        q["g0"] = [toss(4, 0, half(1 - core), gn, other)]
+        q["p0"] = fold_near(2, piece, fp)
+
+    def inner_far():
+        arrive(q["g0"])
+        gr[0] = half(core)[...] + gn[...]
+        q["g0"] = [toss(4, k, gr.at[0], gr.at[k], lax.rem(x + k, nx) * cores + core) for k in range(1, nx)]
+
+    def strip_far():
+        q["p0"] = fold_far(2, q["p0"], piece, fp, tp, rp)
+
+    def inner_row():
+        total = fold_end(q["g0"], gr)
+        gc[...] = total
+        both_ref[core, urow(r)] = total
+        q["g"] = row_stage(3, lambda p: gc, cslot(r))
+
+    def top_back():
+        arrive(q["t1"])
+        total = None
+        for i in range(nx):
+            for k in range(nr):
+                total = tt[i, k] if total is None else total + tt[i, k]
+        top_ref[c, r] = total
+        q["t2"] = wide(1, lambda i, p: top_ref.at[c, r], top_ref.at[c, r])
+
+    def top_twin():
+        arrive(q["t2"])
+        mine = [top_ref.at[i * cores + core] for i in range(nx)]
+        q["t3"] = [toss(3, nx + i, ref, ref, other) for i, ref in enumerate(mine)]
+
+    def strip_end():
+        strip_ref[...] = fold_end(q["p0"], rp)
+
+    def swap():
+        arrive(q["g"])
+        q["g2"] = toss(4, nx, both_ref.at[core], both_ref.at[core], other)
+
+    far_first = hops[::-1] + [0]
+    up[0][0]()
+    up[1][0]()
+    up[0][1]()
+    lower()
+    for k in far_first:
+        spill(k)
+    up[1][1]()
+    for k in far_first[:1]:
+        pile(k)
+    up[0][2]()
+    for k in far_first[1:]:
+        pile(k)
+    up[1][2]()
     up[0][3]()
     up[1][3]()
-    for i in range(cols // width):
-        here = slice(i * width, (i + 1) * width)
-        un, uo = split(xu[0, :, :, here].reshape(width, width)), split(xu[1, :, :, here].reshape(width, width))
-        vh[:width, here], vl[:width, here] = split(mul(iuo, uo) - mul(mix_u, un))
-        vh[width:, here], vl[width:, here] = split(mul(iun, un))
-    for i in range(rows // width):
-        here = slice(i * width, (i + 1) * width)
-        ps[here] = -mul((ah[here], al[here]), (vh[:width], vl[:width]), NT)
-    pt[...] = -mul(lns, split(ps[...]))
-    each = width // nc
-    part = lambda p: pt.at[pl.ds(pl.multiple_of(p * each, each), each)]
-    piece = lambda p: ps.at[lrow(p)]
-    t0 = fold_near(3, part, nt)
-    t0 = fold_far(3, t0, part, nt, ft, rt)
-    arrive([b1[k] for k in hops])
-    band = rz[0]
-    for k in hops:
-        band = band + rz[k]
-    bc[...] = band
-    bslot = lambda i: band_ref.at[urow(i)]
-    b2 = gather(2, bc, bslot, False)
-    band_ref[urow(r)] = band
-    gp[...] = -mul(split(band), (vh[...], vl[...]), NT)
-    half = lambda i: gp.at[:, pl.ds(pl.multiple_of(i * width, width), width)]
-    g0 = [toss(4, 0, half(1 - core), gn, other)]
-    p0 = fold_near(2, piece, fp)
-    arrive(g0)
-    mine = half(core)[...] + gn[...]
-    gr[0] = mine
-    g0 = [toss(4, k, gr.at[0], gr.at[k], lax.rem(x + k, nx) * cores + core) for k in range(1, nx)]
-    p0 = fold_far(2, p0, piece, fp, tp, rp)
-    total = fold_end(t0, rt)
-    few = each // nr
-    for i in range(nr):
-        st[i] = total[i * few : (i + 1) * few]
-    t1 = row_stage(6, lambda p: st.at[p], tt.at[r])
-    tt[r] = st[r]
-    total = fold_end(g0, gr)
-    gc[...] = total
-    cslot = lambda i: both_ref.at[core, urow(i)]
-    g1 = gather(3, gc, cslot, True)
-    both_ref[core, urow(r)] = total
-    b2[0]()
-    b2[1]()
-    arrive(t1)
-    total = tt[0]
-    for i in range(1, nr):
-        total = total + tt[i]
-    gt[r] = total
-    t2 = row_stage(7, lambda p: gt.at[r], gt.at[r])
-    g1[0]()
-    g1[1]()
-    b2[2]()
-    g1[2]()
-    strip_ref[...] = fold_end(p0, rp)
-    arrive(t2)
-    tslot = lambda i: top_ref.at[i]
-    t3 = spread_start(5, gt, tslot)
-    top_ref[c] = gt[...]
-    g1[3]()
-    g2 = toss(4, nx, both_ref.at[core], both_ref.at[core], other)
-    t3 = spread_end(5, t3, tslot)
-    b2[3]()
-    arrive(t3)
-    arrive([g2])
+    band()
+    upper()
+    top_far()
+    inner()
+    inner_far()
+    strip_far()
+    q["b"][0]()
+    q["b"][1]()
+    inner_row()
+    top_back()
+    q["b"][2]()
+    top_twin()
+    swap()
+    strip_end()
+    q["b"][3]()
+    arrive(q["t3"])
+    arrive([q["g2"]])
     for copy in sent:
         copy.wait_send()
 
@@ -352,7 +399,7 @@
     hbm = pl.BlockSpec(memory_space=pltpu.HBM)
     V, D = pltpu.VMEM, pltpu.SemaphoreType.DMA
     lanes = max(nr, 3 + (2 + nz) * ny)
-    whole = V((nr, each // nr, width), f32)
+    whole = V((nc // 2, nr, each // nr, width), f32)
     operands = (an, un, uo, ln.T, lo.T, lot, uol, iln, iun, ilo, iuo)
     strip, band, both, top = pl.pallas_call(
         functools.partial(kernel, nr, nc, ny),
@@ -369,9 +416,9 @@
             V((nz, ny, hu, cols), f32), V((nz, hu, cols), f32), V((nz, hu, cols), f32),
             *[V((nc // 2, wl, width), f32)] * 3, V((hu, cols), f32),
             V((hu, 2 * width), f32), V((hu, width), f32), V((nc // 2, hu, width), f32), V((hu, width), f32),
-            V((width, width), f32), *[V((nc // 2, each, width), f32)] * 3, whole, whole, whole,
+            V((width, width), f32), V((nc // 2, each, width), f32), whole, whole,
             V((6, width, width), f32),
-            D, D((6,)), D((4,)), D((8, lanes)), D((8, lanes)), D((6, nc)), D((6, nc)),
+            D, D((6,)), D((4,)), D((6, lanes)), D((6, lanes)), D((6, nc)), D((6, nc)), D((2, nc // 2 * nr)), D((2, nc // 2 * nr)),
         ],
         compiler_params=pltpu.CompilerParams(collective_id=0, has_side_effects=True, vmem_limit_bytes=LIMIT),
     )(*[pltpu.with_memory_space_constraint(v, pltpu.HBM) for v in operands])

time: 71.3 us -> 65.8 us (0.923)
  Pallas kernels: 70.5 us -> 65 us
    pallas_call x1, Pallas kernels: 69.2 us -> 63.7 us  [body(): pl.pallas_call(functools.partial(kernel, nr, nc, ny), out_shape=(V((wl, w...]
where the time goes in v6:
time: 65.8 us; the launch traced here: 65.7 us
  Pallas kernels  65 us (99%)
    pallas_call x1, Pallas kernels, body(): pl.pallas_call(functools.partial(kernel, nr, nc, ny), out_shape=(V((wl, w...  63.7 us

profile of v6, /device:TPU:0, one launch (start us, length us, event | category | flops | bytes accessed | tf_op | source)
XLA Modules:
  0.0 65.7 jit_solution(17323184783955022592)
XLA Ops:
  0.6 63.7 %shard_map.146 = (f32[128,256]{1,0:T(8,128)S(1)}, f32[256,1024]{1,0:T(8,128)S(1)}, f32[2,256,256]{2,1,0:T(8,128)S(1)}, f32[4,8,8,256]{3,2,1,0:T(8,128)S(1)}) custom-call(f32[512,1024]{1,0:T(8,128)} %a_hbm.1, f32[32,1024]{1,0:T(8,128)} %un_hbm.1, f32[32,1024]{1,0:T(8,128)} %uo_hbm.1, f32[64,512]{1,0:T(8,128)} %bitcast.4, f32[64,512]{1,0:T(8,128)} %bitcast.5, ...), custom_call_target="tpu_custom_call" | custom-call | tf_op jit(solution)/shard_map/pallas_call | solution.py:404
  64.4 1.3 %shard_map.147 = (f32[256,256]{1,0:T(8,128)}, f32[256,256]{1,0:T(8,128)}, f32[128,256]{1,0:T(8,128)}, f32[256,256]{1,0:T(8,128)}, f32[256,1024]{1,0:T(8,128)}) custom-call(f32[128,256]{1,0:T(8,128)S(1)} %get-tuple-element.9.strip_ref, f32[256,1024]{1,0:T(8,128)S(1)} %get-tuple-element.10.band_ref, f32[2,256,256]{2,1,0:T(8,128)S(1)} %get-tuple-element.11.both_ref, ...), custom_call_target="tpu_custom_call" | custom-call | tf_op jit(solution)/shard_map/pallas_call | solution.py:426

commit v7 on v6

--- a/solution.py
+++ b/solution.py
@@ -43,7 +43,7 @@
     strip_ref, band_ref, both_ref, top_ref,
     a_ref, ah, al, xu, xl, vh, vl, pb, ps, ry, sz, rz, fp, tp, rp, bc, gp, gn, gr, gc,
     pt, nt, st, tt, sq,
-    asem, qsem, osem, rs_send, rs_recv, cs_send, cs_recv, ws_send, ws_recv,
+    asem, qsem, osem, rs_send, rs_recv, cs_send, cs_recv, ws_send, ws_recv, ready,
 ):
     r, c = lax.axis_index("row"), lax.axis_index("col")
     rows, cols = a_hbm.shape
@@ -73,11 +73,12 @@
         copy.start()
     load.start()
     barrier = pltpu.get_barrier_semaphore()
-    for d in range(1, nr):
-        pl.semaphore_signal(barrier, inc=1, device_id={"row": lax.rem(r + d, nr)}, device_id_type=pl.DeviceIdType.MESH)
-    for d in range(1, nc):
-        pl.semaphore_signal(barrier, inc=1, device_id={"col": lax.rem(c + d, nc)}, device_id_type=pl.DeviceIdType.MESH)
-    pl.semaphore_wait(barrier, nr + nc - 2)
+    friends = [{"row": reach(k) * ny + y} for k in ((1, 2) if nz == 4 else hops)]
+    friends += [{"row": z * ny + lax.rem(y + d, ny)} for d in range(1, ny)]
+    friends += [{"col": x * cores + 1 - core}] + [{"col": lax.rem(x + k, nx) * cores + core} for k in range(1, nx)]
+    for friend in friends:
+        pl.semaphore_signal(barrier, inc=1, device_id=friend, device_id_type=pl.DeviceIdType.MESH)
+    pl.semaphore_wait(barrier, len(friends))
 
     def lrow(i):
         return pl.ds(pl.multiple_of(i * wl, wl), wl)
@@ -246,7 +247,8 @@
         zt = reach(k) if k else z
         peers = [zt * ny + lax.rem(y + d, ny) for d in range(1, ny)]
         b0[k] = [
-            push(4, k * ny + d, pb.at[urow(p)], ry.at[k, d], z * ny + lax.rem(y + d, ny)) for d, p in enumerate(peers, 1)
+            push(4, k * ny + d, pb.at[urow(p)], ry.at[k, d], z * ny + lax.rem(y + d, ny))
+            for d, p in enumerate(peers, 1)
         ]
 
     def pile(k):
@@ -261,35 +263,6 @@
         else:
             rz[0] = total
 
-    def upper():
-        for i in range(cols // width):
-            here = slice(i * width, (i + 1) * width)
-            un, uo = split(xu[0, :, :, here].reshape(width, width)), split(xu[1, :, :, here].reshape(width, width))
-            vh[:width, here], vl[:width, here] = split(mul(iuo, uo) - mul(mix_u, un))
-            vh[width:, here], vl[width:, here] = split(mul(iun, un))
-        for i in range(rows // width):
-            here = slice(i * width, (i + 1) * width)
-            ps[here] = -mul((ah[here], al[here]), (vh[:width], vl[:width]), NT)
-        pt[...] = -mul(q["lns"], split(ps[...]))
-        q["t0"] = fold_near(3, part, nt)
-
-    def wide(stage, source, target):
-        out = []
-        for n in range(1, nx * nr):
-            qx, p = lax.rem(x + n // nr, nx), lax.rem(r + n % nr, nr)
-            peer = {"row": p, "col": qx * cores + core}
-            out.append(put(None, peer, source(qx, p), target, ws_send.at[stage, n], ws_recv.at[stage, n]))
-        return out
-
-    def top_far():
-        arrive(q["t0"])
-        for i in range(nx):
-            total = part(i * cores + core)[...] + nt[i]
-            for k in range(nr):
-                st[i, k] = total[k * few : (k + 1) * few]
-        q["t1"] = wide(0, lambda i, p: st.at[i, p], tt.at[x, r])
-        tt[x, r] = st[x, r]
-
     def band():
         arrive([b1[k] for k in hops])
         total = rz[0]
@@ -298,6 +271,44 @@
         bc[...] = total
         band_ref[urow(r)] = total
         q["b"] = gather(2, bc, lambda i: band_ref.at[urow(i)], False)
+
+    def upper():
+        for i in range(cols // width):
+            here = slice(i * width, (i + 1) * width)
+            un, uo = split(xu[0, :, :, here].reshape(width, width)), split(xu[1, :, :, here].reshape(width, width))
+            vh[:width, here], vl[:width, here] = split(mul(iuo, uo) - mul(mix_u, un))
+        for i in range(rows // width):
+            here = slice(i * width, (i + 1) * width)
+            ps[here] = -mul((ah[here], al[here]), (vh[:width], vl[:width]), NT)
+        pt[...] = -mul(q["lns"], split(ps[...]))
+        q["t0"] = fold_near(3, part, nt)
+        for i in range(cols // width):
+            here = slice(i * width, (i + 1) * width)
+            un = split(xu[0, :, :, here].reshape(width, width))
+            vh[width:, here], vl[width:, here] = split(mul(iun, un))
+
+    def wide(stage, source, target):
+        out = []
+        for n in range(1, nx * nr):
+            qx, p = lax.rem(x + n // nr, nx), lax.rem(r + n % nr, nr)
+            peer = {"row": p, "col": qx * cores + core}
+            out.append(put(None, peer, source(qx, p), target, ws_send.at[stage, n], ws_recv.at[stage, n]))
+        return out
+
+    def tell():
+        for k in range(1, nx):
+            peer = lax.rem(x + k, nx) * cores + core
+            pl.semaphore_signal(ready, inc=1, device_id={"col": peer}, device_id_type=pl.DeviceIdType.MESH)
+
+    def top_far():
+        pl.semaphore_wait(ready, nx - 1)
+        arrive(q["t0"])
+        for i in range(nx):
+            total = part(i * cores + core)[...] + nt[i]
+            for k in range(nr):
+                st[i, k] = total[k * few : (k + 1) * few]
+        q["t1"] = wide(0, lambda i, p: st.at[i, p], tt.at[x, r])
+        tt[x, r] = st[x, r]
 
     def inner():
         gp[...] = -mul(split(bc[...]), (vh[...], vl[...]), NT)
@@ -355,6 +366,7 @@
     up[1][2]()
     up[0][3]()
     up[1][3]()
+    tell()
     band()
     upper()
     top_far()
@@ -418,7 +430,7 @@
             V((hu, 2 * width), f32), V((hu, width), f32), V((nc // 2, hu, width), f32), V((hu, width), f32),
             V((width, width), f32), V((nc // 2, each, width), f32), whole, whole,
             V((6, width, width), f32),
-            D, D((6,)), D((4,)), D((6, lanes)), D((6, lanes)), D((6, nc)), D((6, nc)), D((2, nc // 2 * nr)), D((2, nc // 2 * nr)),
+            D, D((6,)), D((4,)), D((6, lanes)), D((6, lanes)), D((6, nc)), D((6, nc)), D((2, nc // 2 * nr)), D((2, nc // 2 * nr)), pltpu.SemaphoreType.REGULAR,
         ],
         compiler_params=pltpu.CompilerParams(collective_id=0, has_side_effects=True, vmem_limit_bytes=LIMIT),
     )(*[pltpu.with_memory_space_constraint(v, pltpu.HBM) for v in operands])

time: 65.8 us -> 64.1 us (0.974)
  Pallas kernels: 65 us -> 63.3 us
    pallas_call x1, Pallas kernels: 63.7 us -> 62 us  [body(): pl.pallas_call(functools.partial(kernel, nr, nc, ny), out_shape=(V((wl, w...]
where the time goes in v7:
time: 64.1 us; the launch traced here: 64 us
  Pallas kernels  63.3 us (99%)
    pallas_call x1, Pallas kernels, body(): pl.pallas_call(functools.partial(kernel, nr, nc, ny), out_shape=(V((wl, w...  62 us
    pallas_call x1, Pallas kernels, body(): pl.pallas_call(finish, out_shape=[jax.ShapeDtypeStruct(shape, f32) for sh...  1.31 us

profile of v7, /device:TPU:0, one launch (start us, length us, event | category | flops | bytes accessed | tf_op | source)
XLA Modules:
  0.0 64.0 jit_solution(16508459685611643646)
XLA Ops:
  0.6 62.0 %shard_map.146 = (f32[128,256]{1,0:T(8,128)S(1)}, f32[256,1024]{1,0:T(8,128)S(1)}, f32[2,256,256]{2,1,0:T(8,128)S(1)}, f32[4,8,8,256]{3,2,1,0:T(8,128)S(1)}) custom-call(f32[512,1024]{1,0:T(8,128)} %a_hbm.1, f32[32,1024]{1,0:T(8,128)} %un_hbm.1, f32[32,1024]{1,0:T(8,128)} %uo_hbm.1, f32[64,512]{1,0:T(8,128)} %bitcast.4, f32[64,512]{1,0:T(8,128)} %bitcast.5, ...), custom_call_target="tpu_custom_call" | custom-call | tf_op jit(solution)/shard_map/pallas_call | solution.py:416
  62.6 1.3 %shard_map.147 = (f32[256,256]{1,0:T(8,128)}, f32[256,256]{1,0:T(8,128)}, f32[128,256]{1,0:T(8,128)}, f32[256,256]{1,0:T(8,128)}, f32[256,1024]{1,0:T(8,128)}) custom-call(f32[128,256]{1,0:T(8,128)S(1)} %get-tuple-element.9.strip_ref, f32[256,1024]{1,0:T(8,128)S(1)} %get-tuple-element.10.band_ref, f32[2,256,256]{2,1,0:T(8,128)S(1)} %get-tuple-element.11.both_ref, ...), custom_call_target="tpu_custom_call" | custom-call | tf_op jit(solution)/shard_map/pallas_call | solution.py:438

commit v8 on v7

--- a/solution.py
+++ b/solution.py
@@ -69,7 +69,7 @@
             [(un_hbm, xu.at[0, r]), (uo_hbm, xu.at[1, r]), (ln_hbm, xl.at[0, c]), (lo_hbm, xl.at[1, c])]
         )
     ]
-    for copy in loads + own:
+    for copy in own + loads:
         copy.start()
     load.start()
     barrier = pltpu.get_barrier_semaphore()
@@ -211,9 +211,11 @@
 
     lslot = [lambda i: xl.at[0, i], lambda i: xl.at[1, i]]
     uslot = [lambda i: xu.at[0, i], lambda i: xu.at[1, i]]
-    low = [spread_start(0, ln_hbm, lslot[0]), spread_start(1, lo_hbm, lslot[1])]
-    up = [gather(0, un_hbm, uslot[0], False), gather(1, uo_hbm, uslot[1], True)]
-    for copy in own + loads:
+    for copy in own:
+        copy.wait()
+    low = [spread_start(0, xl.at[0, c], lslot[0]), spread_start(1, xl.at[1, c], lslot[1])]
+    up = [gather(0, xu.at[0, r], uslot[0], False), gather(1, xu.at[1, r], uslot[1], True)]
+    for copy in loads:
         copy.wait()
     iuo, iun = split(sq[0]), split(sq[2])
     mix_u = split(mul(split(mul(iuo, split(sq[1]))), iun))
@@ -350,7 +352,7 @@
         arrive(q["g"])
         q["g2"] = toss(4, nx, both_ref.at[core], both_ref.at[core], other)
 
-    far_first = hops[::-1] + [0]
+    far_first = hops[nz // 2 - 1 : nz // 2] + [k for k in hops[::-1] if k != nz // 2] + [0]
     up[0][0]()
     up[1][0]()
     up[0][1]()
@@ -372,11 +374,11 @@
     top_far()
     inner()
     inner_far()
-    strip_far()
     q["b"][0]()
     q["b"][1]()
+    top_back()
     inner_row()
-    top_back()
+    strip_far()
     q["b"][2]()
     top_twin()
     swap()

time: 64.1 us -> 63.5 us (level)
  no operation moved by 1% of the time
where the time goes in v8:
time: 63.5 us; the launch traced here: 63.4 us
  Pallas kernels  62.7 us (99%)
  between operations  0.64 us (1%)
    pallas_call x1, Pallas kernels, body(): pl.pallas_call(functools.partial(kernel, nr, nc, ny), out_shape=(V((wl, w...  61.4 us
    pallas_call x1, Pallas kernels, body(): pl.pallas_call(finish, out_shape=[jax.ShapeDtypeStruct(shape, f32) for sh...  1.31 us

profile of v8, /device:TPU:0, one launch (start us, length us, event | category | flops | bytes accessed | tf_op | source)
XLA Modules:
  0.0 63.4 jit_solution(2166163264234171039)
XLA Ops:
  0.6 61.4 %shard_map.146 = (f32[128,256]{1,0:T(8,128)S(1)}, f32[256,1024]{1,0:T(8,128)S(1)}, f32[2,256,256]{2,1,0:T(8,128)S(1)}, f32[4,8,8,256]{3,2,1,0:T(8,128)S(1)}) custom-call(f32[512,1024]{1,0:T(8,128)} %a_hbm.1, f32[32,1024]{1,0:T(8,128)} %un_hbm.1, f32[32,1024]{1,0:T(8,128)} %uo_hbm.1, f32[64,512]{1,0:T(8,128)} %bitcast.4, f32[64,512]{1,0:T(8,128)} %bitcast.5, ...), custom_call_target="tpu_custom_call" | custom-call | tf_op jit(solution)/shard_map/pallas_call | solution.py:418
  62.1 1.3 %shard_map.147 = (f32[256,256]{1,0:T(8,128)}, f32[256,256]{1,0:T(8,128)}, f32[128,256]{1,0:T(8,128)}, f32[256,256]{1,0:T(8,128)}, f32[256,1024]{1,0:T(8,128)}) custom-call(f32[128,256]{1,0:T(8,128)S(1)} %get-tuple-element.9.strip_ref, f32[256,1024]{1,0:T(8,128)S(1)} %get-tuple-element.10.band_ref, f32[2,256,256]{2,1,0:T(8,128)S(1)} %get-tuple-element.11.both_ref, ...), custom_call_target="tpu_custom_call" | custom-call | tf_op jit(solution)/shard_map/pallas_call | solution.py:440
